TPU v7x, 128 devices: a whole 4x4x4 slice. The times are simulated.
128 devices in a mesh: row: 8 (over z, core), col: 16 (over x, y).
Axes of the slice: x: 4, y: 4, z: 4, core: 2. Of those that a mesh axis runs over, the one named last changes fastest.
Arguments:
- reflection: bfloat16 [2, 1024, 16384], P(None, 'col', 'row'), may hold values from -6 to 6
- focus_in: bfloat16 [2, 16384, 8192], P(None, 'row', 'col'), may hold values from -1 to 1
- focus_out: bfloat16 [2, 8192, 1024], P(None, 'row'), may hold values from -1 to 1
- ref_angle: float32 [8192, 8192], P('row', 'col'), may hold values from -3.140625 to 3.140625
- element_order: int32 [16384], P('row'), may hold values from 0 to 16383, as said below
- q_start: bfloat16 [8192, 2, 256], P('row'), may hold values from -1 to 1
Outputs:
- basis: float32 [8192, 2, 256], P(('row', 'col'))
Inputs may be any that keep to these rules, and one draw needn't show every extreme that they name: `element_order`: a permutation of 0 to 16383 that maps each aligned block of 512 positions onto the same block.
All inputs are finite; a program needn't handle non-finite values.
Results may differ from a plain program's by a relative error of at most 0.0047.
Values may be sent and summed in bfloat16 or wider, within the bound.
A program may use at most 192 MiB of HBM per device.

v0:
```python
import math

import jax
import jax.numpy as jnp
from jax import lax
from jax.sharding import PartitionSpec as P

NF = 8192


def cross(left_re, left_im, right_re, right_im):
    real_part = jnp.dot(left_re, right_re, preferred_element_type=jnp.float32) - jnp.dot(
        left_im, right_im, preferred_element_type=jnp.float32
    )
    imag_part = jnp.dot(left_re, right_im, preferred_element_type=jnp.float32) + jnp.dot(
        left_im, right_re, preferred_element_type=jnp.float32
    )
    return (real_part, imag_part)


def tdot(left, right, precision=None):
    return lax.dot_general(
        left,
        right,
        (((0,), (0,)), ((), ())),
        precision=precision,
        preferred_element_type=jnp.float32,
    )


def adjoint_product(left_re, left_im, right_re, right_im, precision=None):
    real_part = tdot(left_re, right_re, precision) + tdot(left_im, right_im, precision)
    imag_part = tdot(left_re, right_im, precision) - tdot(left_im, right_re, precision)
    return (real_part, imag_part)


def orthonormal(image_re, image_im, gram_re, gram_im, scale):
    order = gram_re.shape[0]
    rows = image_re.shape[0]
    upper_half = jnp.stack([gram_re, gram_im], axis=-1)
    lower_half = jnp.stack([-gram_im, gram_re], axis=-1)
    embedded = jnp.stack([upper_half, lower_half], axis=1).reshape(2 * order, 2 * order)
    factor = jnp.linalg.cholesky(embedded)
    image_flat = jnp.stack([image_re, image_im], axis=-1).reshape(rows, 2 * order)
    solved = lax.linalg.triangular_solve(
        factor, image_flat, left_side=False, lower=True, transpose_a=True
    )
    paired = solved.reshape(rows, order, 2) * scale
    return jnp.stack([paired[:, :, 0], paired[:, :, 1]], axis=1)


def body(reflection, focus_in, focus_out, ref_angle, element_order, q_start):
    local_inputs = focus_in.shape[1]
    ordered = jnp.take(focus_in, element_order % local_inputs, axis=1)
    piece = lax.all_gather(reflection, "col", axis=1, tiled=True)
    part_re, part_im = cross(piece[0], piece[1], ordered[0], ordered[1])
    terms = jnp.stack([part_re, part_im])
    focused = lax.psum(terms, "row").astype(jnp.bfloat16)
    outer_re, outer_im = cross(focus_out[0], focus_out[1], focused[0], focused[1])
    cosine = jnp.cos(ref_angle)
    sine = jnp.sin(ref_angle)
    dense_re = (outer_re * cosine + outer_im * sine).astype(jnp.bfloat16)
    dense_im = (outer_im * cosine - outer_re * sine).astype(jnp.bfloat16)
    adj_re, adj_im = adjoint_product(dense_re, dense_im, q_start[:, 0], q_start[:, 1])
    adj_re, adj_im = lax.psum((adj_re, adj_im), "row")
    adj_re = adj_re.astype(jnp.bfloat16)
    adj_im = adj_im.astype(jnp.bfloat16)
    share_rows = dense_re.shape[0] // lax.axis_size("col")
    product_precision = lax.Precision.DEFAULT
    image_re, image_im = cross(dense_re, dense_im, adj_re, adj_im)
    image_re, image_im = lax.psum((image_re, image_im), "col")
    gram_re, gram_im = adjoint_product(image_re, image_im, image_re, image_im, product_precision)
    gram_re, gram_im = lax.psum((gram_re, gram_im), "row")
    offset = lax.axis_index("col") * share_rows
    image_re = lax.dynamic_slice_in_dim(image_re, offset, share_rows, 0)
    image_im = lax.dynamic_slice_in_dim(image_im, offset, share_rows, 0)
    return orthonormal(image_re, image_im, gram_re, gram_im, math.sqrt(NF))


def solution(mesh):
    in_specs = (
        P(None, "col", "row"),
        P(None, "row", "col"),
        P(None, "row", None),
        P("row", "col"),
        P("row"),
        P("row", None, None),
    )
    out_specs = P(("row", "col"), None, None)
    return jax.shard_map(body, mesh=mesh, in_specs=in_specs, out_specs=out_specs, check_vma=False)
```

profile of v0, /device:TPU:0, one launch (start us, length us, event | category | flops | bytes accessed | tf_op | source)
XLA Modules:
  0.0 608.9 jit_solution(14751855602636319297)
XLA Ops:
  6.5 0.7 all-gather.2.cloned.1.call-update
  7.3 1.9 copy.22
  9.3 46.5 %gather_fusion = bf16[2048,2,512]{2,0,1:T(8,128)(2,1)} fusion(bf16[2,2048,512]{2,1,0:T(8,128)(2,1)} %param.7, s32[2048]{0:T(1024)S(1)} %broadcast_clamp_fusion), kind=kCustom, calls=%fused_computation | custom fusion | bytes 8396800 | tf_op jit(solution)/shard_map/jit(_take)/gather | solution.py:54
  55.8 8.2 %fusion.67 = (f32[1024,512]{0,1:T(8,128)}, f32[1024,512]{0,1:T(8,128)}) fusion(f32[1024,512]{0,1:T(8,128)S(1)} %copy.22), kind=kLoop, calls=%fused_computation.136 | loop fusion | bytes 6291456 | tf_op jit(solution)/shard_map/cos | solution.py:60
  64.0 2.3 fusion.68
  66.6 2.8 select_bitcast_fusion
  69.4 13.3 %all-gather.2.cloned.1.call-done = bf16[2,1024,2048]{2,1,0:T(8,128)(2,1)} async-done(((bf16[2,64,2048]{2,1,0:T(8,128)(2,1)}), bf16[2,1024,2048]{2,1,0:T(8,128)(2,1)}) %all-gather.2.cloned.1.call-update) | async-done | bytes 8388624 | tf_op jit(solution)/shard_map/all_gather | solution.py:55
  82.7 5.3 fusion
  88.1 1.1 copy-done.11
  89.2 2.4 fusion.1
  91.6 2.4 add_bitcast_fusion
  94.0 2.4 subtract_bitcast_fusion
  96.4 2.5 pad_maximum_fusion
  98.8 58.7 %all-reduce.12 = bf16[2,1024,512]{1,2,0:T(8,128)(2,1)S(1)} all-reduce(f32[2,1024,512]{1,2,0:T(8,128)} %pad_maximum_fusion), channel_id=1, replica_groups=mesh['row'=8,'col'=16] {'row'}, use_global_device_ids=true, to_apply=%region_0.1 | all-reduce | flops 1048576 | bytes 6291456 | tf_op jit(solution)/shard_map/psum | solution.py:58
  157.6 3.7 fusion.10
  161.3 1.3 fusion.8
  162.6 1.3 fusion.20
  164.2 0.6 copy-done.4
  164.8 3.0 fusion.7
  167.9 0.4 fusion.30
  168.3 0.8 copy-done.8
  169.1 0.4 fusion.29
  169.5 1.2 convolution_subtract_fusion.1
  170.7 1.2 convolution_add_fusion.1
  172.0 51.7 %all-reduce.13 = (bf16[512,256]{1,0:T(8,128)(2,1)S(1)}, bf16[512,256]{1,0:T(8,128)(2,1)S(1)}) all-reduce(f32[512,256]{1,0:T(8,128)} %convolution_subtract_fusion.1, f32[512,256]{1,0:T(8,128)} %convolution_add_fusion.1), channel_id=1, replica_groups=mesh['row'=8,'col'=16] {'row'}, use_global_device_ids=true, to_apply=%region_2.3 | all-reduce | flops 262144 | bytes 1572864 | tf_op jit(solution)/shard_map/psum | solution.py:65
  223.6 0.5 fusion.73
  224.1 0.5 fusion.74
  224.6 1.5 convolution_add_fusion
  226.1 1.4 convolution_subtract_fusion
  227.6 89.7 %all-reduce.9.cloned.1.call-done = (f32[1024,256]{1,0:T(8,128)}, f32[1024,256]{1,0:T(8,128)}) async-done(((f32[1024,256]{1,0:T(8,128)}, f32[1024,256]{1,0:T(8,128)}), (f32[1024,256]{1,0:T(8,128)}, f32[1024,256]{1,0:T(8,128)})) %all-reduce.9.cloned.1.call-update) | async-done | bytes 2097168 | tf_op jit(solution)/shard_map/psum | solution.py:71
  317.3 2.1 fusion.71
  319.5 0.3 fusion.72
  319.9 1.0 fusion.26
  320.9 1.0 convolution_subtract_fusion.2
  322.4 60.8 %all-reduce.11.cloned.1.call-done = (f32[256,256,1]{1,0,2:T(8,128)}, f32[256,256]{1,0:T(8,128)}) async-done(((f32[256,256,1]{1,0,2:T(8,128)}, f32[256,256]{1,0:T(8,128)}), (f32[256,256,1]{1,0,2:T(8,128)}, f32[256,256]{1,0:T(8,128)})) %all-reduce.11.cloned.1.call-update) | async-done | bytes 524304 | tf_op jit(solution)/shard_map/psum | solution.py:73
  383.2 1.0 negate_bitcast_fusion
  384.2 1.2 maximum_bitcast_fusion
  385.5 31.5 %copy.27 = f32[256,2,256,2]{3,2,1,0:T(8,128)} copy(f32[256,2,256,2]{2,0,3,1:T(8,128)S(1)} %pad_maximum_fusion.1) | data formatting | bytes 2097152 | tf_op jit(solution)/shard_map/stack | solution.py:42
  417.0 47.4 %reshape.50 = f32[512,512]{1,0:T(8,128)S(1)} reshape(f32[256,2,256,2]{3,2,1,0:T(8,128)} %copy.27) | data formatting | bytes 2097152 | tf_op jit(solution)/shard_map/reshape | solution.py:42
  464.4 0.3 copy.28
  465.0 11.7 %cholesky.104 = f32[128,128]{1,0:T(8,128)S(1)} custom-call(f32[128,128]{1,0:T(8,128)S(1)} %cholesky.266), custom_call_target="Cholesky" | custom-call | tf_op jit(solution)/shard_map/jit(cholesky)/cholesky | solution.py:43
  476.9 9.8 %custom-call.30 = f32[1,128,128]{1,2,0:T(8,128)S(1)} custom-call(f32[1,128,128]{2,1,0:T(8,128)S(1)} %get-tuple-element.51), custom_call_target="InvertDiagBlocksLowerTriangular" | custom-call | tf_op jit(solution)/shard_map/jit(cholesky)/cholesky | solution.py:43
  487.4 11.7 %cholesky.217 = f32[128,128]{1,0:T(8,128)S(1)} custom-call(f32[128,128]{1,0:T(8,128)S(1)} %cholesky.270), custom_call_target="Cholesky" | custom-call | tf_op jit(solution)/shard_map/jit(cholesky)/cholesky | solution.py:43
  499.1 10.0 %custom-call.31 = f32[1,128,128]{1,2,0:T(8,128)S(1)} custom-call(f32[1,128,128]{2,1,0:T(8,128)S(1)} %get-tuple-element.48), custom_call_target="InvertDiagBlocksLowerTriangular" | custom-call | tf_op jit(solution)/shard_map/jit(cholesky)/cholesky | solution.py:43
  509.4 0.4 convolution_subtract_fusion.4
  509.8 11.7 %cholesky.238 = f32[128,128]{1,0:T(8,128)S(1)} custom-call(f32[128,128]{1,0:T(8,128)S(1)} %cholesky.275), custom_call_target="Cholesky" | custom-call | tf_op jit(solution)/shard_map/jit(cholesky)/cholesky | solution.py:43
  521.5 9.8 %custom-call.32 = f32[1,128,128]{1,2,0:T(8,128)S(1)} custom-call(f32[1,128,128]{2,1,0:T(8,128)S(1)} %get-tuple-element.45), custom_call_target="InvertDiagBlocksLowerTriangular" | custom-call | tf_op jit(solution)/shard_map/jit(cholesky)/cholesky | solution.py:43
  531.5 0.4 convolution_subtract_fusion.5
  531.9 11.7 %cholesky.255 = f32[128,128]{1,0:T(8,128)S(1)} custom-call(f32[128,128]{1,0:T(8,128)S(1)} %convolution_subtract_fusion.5), custom_call_target="Cholesky" | custom-call | tf_op jit(solution)/shard_map/jit(cholesky)/cholesky | solution.py:43
  543.7 0.6 compare_reduce_fusion.1
  544.3 0.7 compare_reduce_fusion
  545.0 0.7 compare_reduce_fusion.2
  548.4 10.7 %while.1 = (s32[]{:T(128)}, f32[512,512]{1,0:T(8,128)S(1)}, s32[4,2]{0,1:T(2,128)S(1)}, f32[4,128,128]{2,1,0:T(8,128)}, s32[]{:T(128)}) while((s32[]{:T(128)}, f32[512,512]{1,0:T(8,128)S(1)}, s32[4,2]{0,1:T(2,128)S(1)}, f32[4,128,128]{2,1,0:T(8,128)}, s32[]{:T(128)}) %tuple.35), condition=%wide.while_cond, body=%wide.while_body.sunk | while | flops 2 | bytes 132205 | solution.py:45
  548.7 0.6 fusion.101
  549.3 2.0 bitcast_dynamic-update-slice_fusion.2
  551.3 0.6 fusion.101
  551.9 2.0 bitcast_dynamic-update-slice_fusion.2
  553.9 0.6 fusion.101
  554.5 2.0 bitcast_dynamic-update-slice_fusion.2
  556.5 0.6 fusion.101
  557.1 2.0 bitcast_dynamic-update-slice_fusion.2
  559.1 40.1 %custom-call.33 = f32[4,128,128]{1,2,0:T(8,128)S(1)} custom-call(f32[4,128,128]{2,1,0:T(8,128)} %get-tuple-element.12), custom_call_target="InvertDiagBlocksLowerTriangular" | custom-call | tf_op jit(solution)/shard_map/triangular_solve | solution.py:45
  600.4 0.4 convolution_subtract_fusion.6
  601.4 0.8 copy.34
  (67 shorter events, 5.0 us)
Async XLA Ops:
  6.5 76.2 %all-gather.2.cloned.1.call-start = ((), (), s32[]{:S(2)}) async-start(), calls=%async_computation | async-start | bytes 8912896 | tf_op jit(solution)/shard_map/all_gather | solution.py:55
  7.3 2.0 copy-start.10
  7.3 310.1 %all-reduce.9.cloned.1.call-start = ((), (), s32[]{:S(2)}) async-start(), calls=%async_computation.1 | async-start | bytes 4194304 | tf_op jit(solution)/shard_map/psum | solution.py:71
  55.8 8.2 %copy-start.7 = (bf16[1024,2,256]{2,1,0:T(2,128)(2,1)S(1)}, bf16[1024,2,256]{2,1,0:T(2,128)(2,1)}, u32[]{:S(2)}) copy-start(bf16[1024,2,256]{2,1,0:T(2,128)(2,1)} %param.11) | copy-start | bytes 3145732
  64.0 2.6 copy-start.2
  82.7 5.4 copy-start.6
  82.7 6.5 %copy-start.11 = (bf16[2,1024,2048]{2,1,0:T(8,128)(2,1)S(1)}, bf16[2,1024,2048]{2,1,0:T(8,128)(2,1)}, u32[]{:S(2)}) copy-start(bf16[2,1024,2048]{2,1,0:T(8,128)(2,1)} %all-gather.2.cloned.1.call-done) | copy-start | bytes 25165828
  157.6 5.0 copy-start.5
  157.6 3.7 copy-start.9
  162.6 1.6 copy-start.3
  162.6 2.2 copy-start.4
  167.8 1.2 copy-start.8
  227.5 155.7 %all-reduce.11.cloned.1.call-start = ((), (), s32[]{:S(2)}) async-start(), calls=%async_computation.2 | async-start | bytes 1048576 | tf_op jit(solution)/shard_map/psum | solution.py:73
  317.3 2.1 copy-start
  317.3 2.2 copy-start.1
Sparse Core Ops, SparseCore 0:
  9.5 73.1 all-gather.1
  227.7 89.6 all-reduce.8
  322.1 61.0 all-reduce.10
where the time goes:
time: 614 us; the launch traced here: 609 us
  waiting for transfers between devices  165 us (27%)
  local copies, waits for them, and re-layouts  154 us (25%)
  other arithmetic  127 us (21%)
  blocking collectives  110 us (18%)
  matrix products  37.1 us (6%)
  between operations  16.4 us (3%)
    psum x1, waiting for transfers between devices, body(): image_re, image_im = lax.psum((image_re, image_im), 'col')  89.7 us
    another operation x14, other arithmetic, orthonormal(): factor = jnp.linalg.cholesky(embedded)  78.6 us
    psum x1, waiting for transfers between devices, body(): gram_re, gram_im = lax.psum((gram_re, gram_im), 'row')  60.8 us
    psum x1, blocking collectives, body(): focused = lax.psum(terms, 'row').astype(jnp.bfloat16)  58.7 us
    psum x1, blocking collectives, body(): adj_re, adj_im = lax.psum((adj_re, adj_im), 'row')  51.7 us
    reshape x2, local copies, waits for them, and re-layouts, orthonormal(): jnp.stack([upper_half, lower_half], axis=1).reshape(2 * order, 2 * order)  47.8 us
    gather x1, local copies, waits for them, and re-layouts, body(): ordered = jnp.take(focus_in, element_order % local_inputs, axis=1)  46.5 us
    another operation x3, other arithmetic, orthonormal(): lax.linalg.triangular_solve(factor, image_flat, left_side=False, lower=Tr...  40.3 us
  transfers between devices with their start and end apart: 3, of which 3 were waited for; matrix products, arithmetic and copies ran while one was open for 10% of the time, Pallas kernels for 0%

commit v1 on v0

v1 whole, which is shorter than its diff:
```python
import functools
import math

import jax
import jax.numpy as jnp
from jax import lax
from jax.experimental import pallas as pl
from jax.experimental.pallas import tpu as pltpu
from jax.sharding import PartitionSpec as P

NF = 8192
PANEL_W = 512
NB = 32
HI = lax.Precision.HIGHEST
RANK=256

def dott(a, b, precision=HI):
    return lax.dot_general(a, b, (((1,), (1,)), ((), ())), precision=precision, preferred_element_type=jnp.float32)

def factor_inverse(diag):
    lane = lax.broadcasted_iota(jnp.int32, (NB, 4 * NB), 1)
    sub = lax.broadcasted_iota(jnp.int32, (NB, 4 * NB), 0)
    unit = (lane - 2 * NB == sub).astype(jnp.float32)
    unit_i = (lane - 3 * NB == sub).astype(jnp.float32)
    re, im = diag[:, :NB], diag[:, NB:]
    z = jnp.zeros((NB, 2 * NB), jnp.float32)
    w = jnp.concatenate([re, im, z], axis=1) + unit
    v = jnp.concatenate([-im, re, z], axis=1) + unit_i
    sub1 = sub[:, :1]
    for j in range(NB - 1):
        piv = w[j : j + 1, j : j + 1]
        below = sub1 > j
        c_re = jnp.where(below, w[:, j : j + 1], 0.0)
        c_im = jnp.where(below, w[:, NB + j : NB + j + 1], 0.0)
        inv = 1.0 / piv
        row = w[j : j + 1, :] * inv
        rov = v[j : j + 1, :] * inv
        w = w - (c_re * row + c_im * rov)
        v = v - (c_re * rov - c_im * row)
    d = jnp.sum(jnp.where(lane == sub, w, 0.0), axis=1, keepdims=True)
    return w[:, 2 * NB :] * lax.rsqrt(d)

def swapped(m):
    return jnp.concatenate([-m[:, NB:], m[:, :NB]], axis=1)

def chol_kernel(scale, g_ref, y_ref, out_ref, a_ref):
    n = RANK
    rows = y_ref.shape[0]
    panels = n // NB
    a_ref[:n, :] = g_ref[...]
    a_ref[n:, :] = y_ref[...]
    for k in range(panels):
        lo = k * NB
        inv = factor_inverse(a_ref[lo : lo + NB, 2 * lo : 2 * lo + 2 * NB])
        both = jnp.concatenate([inv, swapped(inv)], axis=0)
        ap = a_ref[lo + NB :, 2 * lo : 2 * lo + 2 * NB]
        low = dott(ap, both)
        x = low[low.shape[0] - rows :] * scale
        out_ref[:, 0, lo : lo + NB] = x[:, :NB]
        out_ref[:, 1, lo : lo + NB] = x[:, NB:]
        left = panels - 1 - k
        if left:
            lk = low[: left * NB]
            sk = swapped(lk)
            q = jnp.concatenate([lk.reshape(left, NB, 2 * NB), sk.reshape(left, NB, 2 * NB)], axis=1)
            q = q.reshape(left * 2 * NB, 2 * NB)
            a_ref[lo + NB :, 2 * lo + 2 * NB :] -= dott(low, q)

def chol(g, y, scale):
    return pl.pallas_call(
        functools.partial(chol_kernel, scale),
        out_shape=jax.ShapeDtypeStruct((y.shape[0], 2, RANK), jnp.float32),
        in_specs=[pl.BlockSpec(memory_space=pltpu.VMEM)] * 2,
        out_specs=pl.BlockSpec(memory_space=pltpu.VMEM),
        scratch_shapes=[pltpu.VMEM((RANK + y.shape[0], 2 * RANK), jnp.float32)],
    )(g, y)

def interleave(re, im):
    r = re.shape[0]
    return jnp.stack([re.reshape(r, -1, NB), im.reshape(r, -1, NB)], axis=2).reshape(r, -1)


def times_i(m):
    r = m.shape[0]
    pairs = m.reshape(r, -1, 2, NB)
    return jnp.stack([-pairs[:, :, 1], pairs[:, :, 0]], axis=2).reshape(r, -1)


def f32dot(a, b, dims, precision=None):
    return lax.dot_general(a, b, ((dims[0], dims[1]), ((), ())), precision=precision, preferred_element_type=jnp.float32)


def body(reflection, focus_in, focus_out, ref_angle, element_order, q_start):
    local_inputs = focus_in.shape[1]
    blocks = local_inputs // PANEL_W
    place = (element_order % PANEL_W).reshape(blocks, PANEL_W)
    onehot = (place[:, :, None] == jnp.arange(PANEL_W, dtype=jnp.int32)).astype(jnp.bfloat16)
    refl = reflection.reshape(2 * reflection.shape[1], blocks, PANEL_W)
    refl = jnp.einsum("mbt,bts->mbs", refl, onehot, preferred_element_type=jnp.float32).astype(jnp.bfloat16)
    refl = refl.reshape(reflection.shape)
    piece = lax.all_gather(refl, "col", axis=1, tiled=True)
    part_re = f32dot(piece[0], focus_in[0], ((1,), (0,))) - f32dot(piece[1], focus_in[1], ((1,), (0,)))
    part_im = f32dot(piece[0], focus_in[1], ((1,), (0,))) + f32dot(piece[1], focus_in[0], ((1,), (0,)))
    focused = lax.psum(jnp.stack([part_re, part_im]), "row").astype(jnp.bfloat16)
    outer_re = f32dot(focus_out[0], focused[0], ((1,), (0,))) - f32dot(focus_out[1], focused[1], ((1,), (0,)))
    outer_im = f32dot(focus_out[0], focused[1], ((1,), (0,))) + f32dot(focus_out[1], focused[0], ((1,), (0,)))
    cosine = jnp.cos(ref_angle)
    sine = jnp.sin(ref_angle)
    dense_re = (outer_re * cosine + outer_im * sine).astype(jnp.bfloat16)
    dense_im = (outer_im * cosine - outer_re * sine).astype(jnp.bfloat16)
    q1 = interleave(q_start[:, 0], q_start[:, 1])
    q2 = interleave(q_start[:, 1], -q_start[:, 0])
    adj = f32dot(dense_re, q1, ((0,), (0,))) + f32dot(dense_im, q2, ((0,), (0,)))
    adj = lax.psum(adj, "row").astype(jnp.bfloat16)
    image = f32dot(dense_re, adj, ((1,), (0,))) + f32dot(dense_im, times_i(adj), ((1,), (0,)))
    image = lax.psum_scatter(image, "col", scatter_dimension=0, tiled=True)
    im_re = image.reshape(-1, RANK // NB, 2, NB)[:, :, 0].reshape(-1, RANK)
    im_im = image.reshape(-1, RANK // NB, 2, NB)[:, :, 1].reshape(-1, RANK)
    gram = f32dot(im_re, image, ((0,), (0,)), HI) - f32dot(im_im, times_i(image), ((0,), (0,)), HI)
    gram = lax.psum(gram, ("row", "col"))
    return chol(gram, image, math.sqrt(NF))


def solution(mesh):
    in_specs = (
        P(None, "col", "row"),
        P(None, "row", "col"),
        P(None, "row", None),
        P("row", "col"),
        P("row"),
        P("row", None, None),
    )
    out_specs = P(("row", "col"), None, None)
    return jax.shard_map(body, mesh=mesh, in_specs=in_specs, out_specs=out_specs, check_vma=False)
```

time: 614 us -> 489 us (0.80)
  local copies, waits for them, and re-layouts: 154 us -> 26.7 us
  other arithmetic: 127 us -> 5.38 us
  waiting for transfers between devices: 165 us -> 272 us
  Pallas kernels: 0 us -> 31 us
  matrix products: 37.1 us -> 28.2 us
    another operation x23 -> x4, other arithmetic: 124 us -> 3.69 us  [the longest x1 2.39 us: body(): jnp.stack([part_re, part_im])]
    reduce_scatter x0 -> x1, waiting for transfers between devices: none -> 73.5 us  [body(): image = lax.psum_scatter(image, 'col', scatter_dimension=0, tiled=True)]
    gather x1 -> x0, local copies, waits for them, and re-layouts: 46.5 us -> none  [body(): ordered = jnp.take(focus_in, element_order % local_inputs, axis=1)]
    reshape x2, local copies, waits for them, and re-layouts: 47.8 us -> 2.6 us  [the longest x1 1.43 us: body(): refl = reflection.reshape(2 * reflection.shape[1], blocks, PANEL_W)]
    another operation x22 -> x2, local copies, waits for them, and re-layouts: 43.1 us -> 2.18 us  [interleave(): jnp.stack([re.reshape(r, -1, NB), im.reshape(r, -1, NB)], axis=2)]
    all_gather x1, waiting for transfers between devices: 13.3 us -> 51.5 us  [body(): piece = lax.all_gather(refl, 'col', axis=1, tiled=True)]
    pallas_call x0 -> x1, Pallas kernels: none -> 31 us  [chol(): pl.pallas_call(functools.partial(chol_kernel, scale), out_shape=jax.Shape...]
    dot_general x20 -> x15, matrix products: 33.5 us -> 28.2 us  [the longest x14 27.3 us: f32dot(): lax.dot_general(a, b, ((dims[0], dims[1]), ((), ())), precision=precision...]
  transfers between devices with their start and end apart: 3 -> 3, of which waited for: 3 -> 3; matrix products, arithmetic and copies ran while one was open for 10% -> 4% of each run, Pallas kernels for 0% -> 0%
where the time goes in v1:
time: 489 us; the launch traced here: 487 us
  waiting for transfers between devices  272 us (56%)
  blocking collectives  110 us (22%)
  Pallas kernels  31 us (6%)
  matrix products  28.2 us (6%)
  local copies, waits for them, and re-layouts  26.7 us (5%)
  between operations  13.4 us (3%)
  other arithmetic  5.38 us (1%)
    psum x1, waiting for transfers between devices, body(): gram = lax.psum(gram, ('row', 'col'))  147 us
    reduce_scatter x1, waiting for transfers between devices, body(): image = lax.psum_scatter(image, 'col', scatter_dimension=0, tiled=True)  73.5 us
    psum x1, blocking collectives, body(): lax.psum(jnp.stack([part_re, part_im]), 'row').astype(jnp.bfloat16)  58.7 us
    all_gather x1, waiting for transfers between devices, body(): piece = lax.all_gather(refl, 'col', axis=1, tiled=True)  51.5 us
    psum x1, blocking collectives, body(): adj = lax.psum(adj, 'row').astype(jnp.bfloat16)  51.1 us
    pallas_call x1, Pallas kernels, chol(): pl.pallas_call(functools.partial(chol_kernel, scale), out_shape=jax.Shape...  31 us
    dot_general x14, matrix products, f32dot(): lax.dot_general(a, b, ((dims[0], dims[1]), ((), ())), precision=precision...  27.3 us
  transfers between devices with their start and end apart: 3, of which 3 were waited for; matrix products, arithmetic and copies ran while one was open for 4% of the time, Pallas kernels for 0%

profile of v1, /device:TPU:0, one launch (start us, length us, event | category | flops | bytes accessed | tf_op | source)
XLA Modules:
  0.0 486.8 jit_solution(17999921471990430603)
XLA Ops:
  6.5 0.0 all-gather.2.cloned.1.call-start
  6.5 0.7 add_select_fusion
  7.3 1.4 reshape.37
  8.7 0.9 fusion.41
  9.6 0.4 copy.11
  10.0 1.2 reshape.38
  11.1 0.0 all-gather.2.cloned.1.call-update
  11.2 0.0 copy-start.2
  11.2 0.0 reduce-scatter.2.cloned.1.call-start
  11.2 2.0 copy.12
  13.2 0.0 copy-done.2
  13.2 2.5 fusion.45
  15.7 2.3 copy.20
  18.1 0.9 neg.18
  19.0 2.3 copy.21
  21.4 1.2 pad_maximum_fusion.2
  22.6 1.1 copy.17
  23.7 1.1 copy.16
  24.8 8.2 %fusion.44 = (f32[1024,512]{0,1:T(8,128)}, f32[1024,512]{0,1:T(8,128)}) fusion(f32[1024,512]{0,1:T(8,128)S(1)} %copy.12), kind=kLoop, calls=%fused_computation.60 | loop fusion | bytes 6291456 | tf_op jit(solution)/shard_map/cos | solution.py:107
  32.9 51.5 %all-gather.2.cloned.1.call-done = bf16[2,1024,2048]{2,1,0:T(8,128)(2,1)} async-done(((bf16[2,64,2048]{2,1,0:T(8,128)(2,1)}), bf16[2,1024,2048]{2,1,0:T(8,128)(2,1)}) %all-gather.2.cloned.1.call-update) | async-done | bytes 8388624 | tf_op jit(solution)/shard_map/all_gather | solution.py:101
  84.5 0.0 copy-start.8
  84.5 0.0 copy-start.9
  84.5 5.3 %fusion.1 = f32[1024,512]{1,0:T(8,128)S(1)} fusion(bf16[2,1024,2048]{2,1,0:T(8,128)(2,1)} %all-gather.2.cloned.1.call-done, bf16[2,2048,512]{2,1,0:T(8,128)(2,1)} %param.7), kind=kOutput, calls=%fused_computation.5 | convolution fusion | flops 2147483648 | bytes 8388608 | tf_op jit(solution)/shard_map/dot_general | solution.py:90
  89.8 0.0 copy-done.8
  89.8 1.1 copy-done.9
  90.9 2.3 fusion.2
  93.2 2.3 add_bitcast_fusion
  95.6 2.3 subtract_bitcast_fusion
  97.9 2.4 pad_maximum_fusion
  100.3 58.7 %all-reduce.5 = bf16[2,1024,512]{2,1,0:T(8,128)(2,1)S(1)} all-reduce(f32[2,1024,512]{2,1,0:T(8,128)} %pad_maximum_fusion), channel_id=1, replica_groups=mesh['row'=8,'col'=16] {'row'}, use_global_device_ids=true, to_apply=%region_0.1 | all-reduce | flops 1048576 | bytes 6291456 | tf_op jit(solution)/shard_map/psum | solution.py:104
  159.0 0.0 copy-start.7
  159.0 3.0 fusion.9
  162.1 0.0 copy-done.7
  162.1 1.3 fusion.11
  163.4 0.0 copy-start
  163.4 0.0 copy-start.1
  163.4 1.3 fusion.34
  164.7 0.2 copy-done
  165.0 0.6 copy-done.1
  165.6 0.0 copy-start.6
  165.6 1.8 fusion.8
  167.5 0.0 copy-start.4
  167.5 0.0 copy-start.3
  167.5 0.0 copy-done.6
  167.5 0.7 fusion.46
  168.2 0.2 copy-done.4
  168.4 0.6 copy-done.3
  169.1 0.8 convolution_add_fusion.1
  169.9 51.1 %all-reduce.6 = bf16[512,512]{1,0:T(8,128)(2,1)S(1)} all-reduce(f32[512,512]{1,0:T(8,128)S(1)} %convolution_add_fusion.1), channel_id=1, replica_groups=mesh['row'=8,'col'=16] {'row'}, use_global_device_ids=true, to_apply=%region_1.2 | all-reduce | flops 262144 | bytes 1572864 | tf_op jit(solution)/shard_map/psum | solution.py:114
  221.0 0.2 copy.18
  221.2 2.0 fusion.47
  223.2 0.1 pad_maximum_fusion.3
  223.3 2.1 convolution_add_fusion
  225.4 0.0 reduce-scatter.2.cloned.1.call-update
  225.4 0.3 all-reduce.4.cloned.1.call-start
  225.7 73.5 %reduce-scatter.2.cloned.1.call-done.y_ref = f32[64,512]{1,0:T(8,128)} async-done(((f32[1024,512]{1,0:T(8,128)}), f32[64,512]{1,0:T(8,128)}) %reduce-scatter.2.cloned.1.call-update) | async-done | bytes 131088 | tf_op jit(solution)/shard_map/reduce_scatter | solution.py:116
  299.2 0.0 copy-start.5
  299.2 1.1 copy.19
  300.4 0.6 fusion.48
  301.0 0.0 copy-done.5
  301.0 1.4 convolution_subtract_fusion
  302.3 0.0 all-reduce.4.cloned.1.call-update
  302.4 146.9 %all-reduce.4.cloned.1.call-done.g_ref = f32[256,512]{1,0:T(8,128)} async-done(((f32[256,512]{1,0:T(8,128)}), f32[256,512]{1,0:T(8,128)}) %all-reduce.4.cloned.1.call-update) | async-done | bytes 524304 | tf_op jit(solution)/shard_map/psum | solution.py:120
  449.3 31.0 %shard_map.64 = f32[64,2,256]{2,1,0:T(2,128)} custom-call(f32[256,512]{1,0:T(8,128)} %all-reduce.4.cloned.1.call-done.g_ref, f32[64,512]{1,0:T(8,128)} %reduce-scatter.2.cloned.1.call-done.y_ref), custom_call_target="tpu_custom_call" | custom-call | tf_op jit(solution)/shard_map/pallas_call | solution.py:70
  (4 shorter events, 0.1 us)
Async XLA Ops:
  6.5 77.9 %all-gather.2.cloned.1.call-start = ((), (), s32[]{:S(2)}) async-start(), calls=%async_computation.1 | async-start | bytes 8912896 | tf_op jit(solution)/shard_map/all_gather | solution.py:101
  11.2 2.1 copy-start.2
  11.2 288.0 %reduce-scatter.2.cloned.1.call-start = ((), (), s32[]{:S(2)}) async-start(), calls=%async_computation.2 | async-start | bytes 2228224 | tf_op jit(solution)/shard_map/reduce_scatter | solution.py:116
  84.5 5.3 %copy-start.8 = (bf16[2,1024,2048]{2,1,0:T(8,128)(2,1)S(1)}, bf16[2,1024,2048]{2,1,0:T(8,128)(2,1)}, u32[]{:S(2)}) copy-start(bf16[2,1024,2048]{2,1,0:T(8,128)(2,1)} %all-gather.2.cloned.1.call-done) | copy-start | bytes 25165828
  84.5 6.4 %copy-start.9 = (bf16[2,2048,512]{2,1,0:T(8,128)(2,1)S(1)}, bf16[2,2048,512]{2,1,0:T(8,128)(2,1)}, u32[]{:S(2)}) copy-start(bf16[2,2048,512]{2,1,0:T(8,128)(2,1)} %param.7) | copy-start | bytes 12582916
  159.0 3.1 copy-start.7
  163.4 1.6 copy-start
  163.4 2.2 copy-start.1
  165.6 1.9 copy-start.6
  167.5 1.0 copy-start.4
  167.5 1.6 copy-start.3
  225.4 223.9 %all-reduce.4.cloned.1.call-start = ((), (), s32[]{:S(2)}) async-start(), calls=%async_computation.3 | async-start | bytes 1048576 | tf_op jit(solution)/shard_map/psum | solution.py:120
  299.2 1.8 copy-start.5
Sparse Core Ops, SparseCore 0:
  11.3 73.1 all-gather.1
  225.5 73.6 reduce-scatter.1
  304.0 145.2 all-reduce.3

commit v2 on v1

--- a/solution.py
+++ b/solution.py
@@ -9,13 +9,206 @@
 from jax.sharding import PartitionSpec as P
 
 NF = 8192
+RANK = 256
 PANEL_W = 512
 NB = 32
 HI = lax.Precision.HIGHEST
-RANK=256
-
-def dott(a, b, precision=HI):
+MESH = pl.DeviceIdType.MESH
+
+
+def dot_nt(a, b, precision=None):
     return lax.dot_general(a, b, (((1,), (1,)), ((), ())), precision=precision, preferred_element_type=jnp.float32)
+
+
+def dot_nn(a, b):
+    return jnp.dot(a, b, preferred_element_type=jnp.float32)
+
+
+def dot_tn(a, b, precision=None):
+    return lax.dot_general(a, b, (((0,), (0,)), ((), ())), precision=precision, preferred_element_type=jnp.float32)
+
+
+def remote(src, dst, send_sem, recv_sem, row, col):
+    return pltpu.make_async_remote_copy(
+        src_ref=src, dst_ref=dst, send_sem=send_sem, recv_sem=recv_sem, device_id=(row, col), device_id_type=MESH
+    )
+
+
+def tail_kernel(
+    dense_re, dense_im, qt_ref, image_ref, gram_ref,
+    zpart, zs1, zr1, zs2, zr2, zfull,
+    yown_a, yown_b, ysa, ysb, yra, yrb, ys2, yr2a, yr2b,
+    hpart, hrecv, hrow,
+    sz1, rz1, sz2, rz2, sz3, rz3, sz4, rz4, sya, rya, syb, ryb, sy2a, ry2a, sy2b, ry2b, sh1, rh1, sh2, rh2, sh3, rh3,
+):
+    r = lax.axis_index("row")
+    c = lax.axis_index("col")
+    z, core = r // 2, r % 2
+    x, y = c // 4, c % 4
+    other = 1 - core
+
+    barrier = pltpu.get_barrier_semaphore()
+    for d in range(1, 8):
+        pl.semaphore_signal(barrier, inc=1, device_id=((r + d) % 8, c), device_id_type=MESH)
+    for d in range(1, 16):
+        pl.semaphore_signal(barrier, inc=1, device_id=(r, (c + d) % 16), device_id_type=MESH)
+
+    half = RANK
+    q1 = qt_ref[...]
+    q2 = jnp.concatenate([q1[half:], -q1[:half]], axis=0)
+    zpart[...] = dot_nn(q1, dense_re[...]) + dot_nn(q2, dense_im[...])
+    pl.semaphore_wait(barrier, 22)
+    zs1[...] = zpart[pl.ds(other * half, half), :].astype(zs1.dtype)
+    pair = remote(zs1, zr1, sz1, rz1, z * 2 + other, c)
+    pair.start()
+    pair.wait_recv()
+    mine = zpart[pl.ds(core * half, half), :] + zr1[...].astype(jnp.float32)
+    quarter = half // 4
+    zs2[...] = mine.reshape(4, quarter, -1).astype(zs2.dtype)
+    zpart[pl.ds(0, half), :] = mine
+    sends = []
+    for d in range(1, 4):
+        to = (z + d) % 4
+        sends.append(remote(zs2.at[to], zr2.at[d - 1], sz2.at[d - 1], rz2.at[d - 1], to * 2 + core, c))
+        sends[-1].start()
+    total = zpart[pl.ds(z * quarter, quarter), :]
+    for d in range(1, 4):
+        sends[d - 1].wait_recv()
+        total = total + zr2[d - 1].astype(jnp.float32)
+    slot = core * half + z * quarter
+    own = zfull.at[pl.ds(slot, quarter), :]
+    zfull[pl.ds(slot, quarter), :] = total.astype(jnp.bfloat16)
+    spread = []
+    for d in range(1, 4):
+        to = (z + d) % 4
+        spread.append(remote(own, own, sz3.at[d - 1], rz3.at[d - 1], to * 2 + core, c))
+        spread[-1].start()
+    relay = [remote(own, own, sz4.at[0], rz4.at[0], z * 2 + other, c)]
+    relay[0].start()
+    for d in range(1, 4):
+        spread[d - 1].wait_recv()
+        origin = (z + 4 - d) % 4
+        part = zfull.at[pl.ds(core * half + origin * quarter, quarter), :]
+        relay.append(remote(part, part, sz4.at[d], rz4.at[d], z * 2 + other, c))
+        relay[-1].start()
+    for d in range(4):
+        relay[d].wait_recv()
+
+    z1 = zfull[...]
+    z2 = jnp.concatenate([-z1[half:], z1[:half]], axis=0)
+    first_a = []
+    for d in (1, 2, 3, 0):
+        to = (x + d) % 4
+        rows = pl.ds(to * 256, 256)
+        block = dot_nt(dense_re[rows, :], z1) + dot_nt(dense_im[rows, :], z2)
+        block_a = block[:, :half].reshape(4, 64, half)
+        block_b = block[:, half:].reshape(4, 64, half)
+        for j in range(4):
+            ysb[j, to] = block_b[j].astype(ysb.dtype)
+            yown_b[j, to] = block_b[j]
+        if d:
+            ysa[d - 1] = block_a.astype(ysa.dtype)
+            first_a.append(remote(ysa.at[d - 1], yra.at[d - 1], sya.at[d - 1], rya.at[d - 1], r, to * 4 + y))
+            first_a[-1].start()
+        else:
+            yown_a[...] = block_a
+    first_b = []
+    for d in range(1, 4):
+        to = (y + d) % 4
+        first_b.append(remote(ysb.at[to], yrb.at[d - 1], syb.at[d - 1], ryb.at[d - 1], r, x * 4 + to))
+        first_b[-1].start()
+    sum_a = yown_a[...]
+    for d in range(1, 4):
+        first_a[d - 1].wait_recv()
+        sum_a = sum_a + yra[d - 1].astype(jnp.float32)
+    yown_a[...] = sum_a
+    ys2[0] = sum_a.astype(ys2.dtype)
+    second_a = []
+    for d in range(1, 4):
+        to = (y + d) % 4
+        second_a.append(remote(ys2.at[0, to], yr2a.at[d - 1], sy2a.at[d - 1], ry2a.at[d - 1], r, x * 4 + to))
+        second_a[-1].start()
+    sum_b = yown_b[y]
+    for d in range(1, 4):
+        first_b[d - 1].wait_recv()
+        sum_b = sum_b + yrb[d - 1].astype(jnp.float32)
+    yown_b[0] = sum_b
+    ys2[1] = sum_b.astype(ys2.dtype)
+    second_b = []
+    for d in range(1, 4):
+        to = (x + d) % 4
+        second_b.append(remote(ys2.at[1, to], yr2b.at[d - 1], sy2b.at[d - 1], ry2b.at[d - 1], r, to * 4 + y))
+        second_b[-1].start()
+    final_a = yown_a[y]
+    for d in range(1, 4):
+        second_a[d - 1].wait_recv()
+        final_a = final_a + yr2a[d - 1].astype(jnp.float32)
+    final_b = yown_b[0, x]
+    for d in range(1, 4):
+        second_b[d - 1].wait_recv()
+        final_b = final_b + yr2b[d - 1].astype(jnp.float32)
+    image_ref[:, :half] = final_a
+    image_ref[:, half:] = final_b
+
+    both = jnp.concatenate([final_a, final_b], axis=0)
+    turned = jnp.concatenate([final_b, -final_a], axis=0)
+    gram_re = dot_tn(both, both, HI)
+    gram_im = dot_tn(both, turned, HI)
+    rows = lax.broadcasted_iota(jnp.int32, (RANK, RANK), 0)
+    cols = lax.broadcasted_iota(jnp.int32, (RANK, RANK), 1)
+    hpart[...] = jnp.where(rows >= cols, gram_re, gram_im).reshape(16, 16, RANK)
+    g1 = []
+    for d in range(1, 16):
+        to = (c + d) % 16
+        g1.append(remote(hpart.at[to], hrecv.at[d - 1], sh1.at[d - 1], rh1.at[d - 1], r, to))
+        g1[-1].start()
+    acc = hpart[c]
+    for d in range(1, 16):
+        g1[d - 1].wait_recv()
+        acc = acc + hrecv[d - 1]
+    hrow[r] = acc
+    g2 = []
+    for d in range(1, 8):
+        g2.append(remote(hrow.at[r], hrow.at[r], sh2.at[d - 1], rh2.at[d - 1], (r + d) % 8, c))
+        g2[-1].start()
+    for d in range(1, 8):
+        g2[d - 1].wait_recv()
+    acc = hrow[0]
+    for i in range(1, 8):
+        acc = acc + hrow[i]
+    gram_ref[c] = acc
+    g3 = []
+    for d in range(1, 16):
+        g3.append(remote(gram_ref.at[c], gram_ref.at[c], sh3.at[d - 1], rh3.at[d - 1], r, (c + d) % 16))
+        g3[-1].start()
+    for d in range(1, 16):
+        g3[d - 1].wait_recv()
+    for copy in [pair] + sends + spread + relay + first_a + first_b + second_a + second_b + g1 + g2 + g3:
+        copy.wait_send()
+
+
+def tail(dense_re, dense_im, qt):
+    bf, f32 = jnp.bfloat16, jnp.float32
+    dma = pltpu.SemaphoreType.DMA
+    vm = pltpu.VMEM
+    scratch = [
+        vm((512, 512), f32), vm((256, 512), bf), vm((256, 512), bf), vm((4, 64, 512), bf), vm((3, 64, 512), bf), vm((512, 512), bf),
+        vm((4, 64, 256), f32), vm((4, 4, 64, 256), f32), vm((3, 4, 64, 256), bf), vm((4, 4, 64, 256), bf),
+        vm((3, 4, 64, 256), bf), vm((3, 4, 64, 256), bf), vm((2, 4, 64, 256), f32), vm((3, 64, 256), f32), vm((3, 64, 256), f32),
+        vm((16, 16, RANK), f32), vm((15, 16, RANK), f32), vm((8, 16, RANK), f32),
+        dma, dma, dma((3,)), dma((3,)), dma((3,)), dma((3,)), dma((4,)), dma((4,)), dma((3,)), dma((3,)), dma((3,)), dma((3,)),
+        dma((3,)), dma((3,)), dma((3,)), dma((3,)), dma((15,)), dma((15,)), dma((7,)), dma((7,)), dma((15,)), dma((15,)),
+    ]
+    vmem = pl.BlockSpec(memory_space=pltpu.VMEM)
+    return pl.pallas_call(
+        tail_kernel,
+        out_shape=(jax.ShapeDtypeStruct((64, 2 * RANK), f32), jax.ShapeDtypeStruct((16, 16, RANK), f32)),
+        in_specs=[vmem] * 3,
+        out_specs=(vmem, vmem),
+        scratch_shapes=scratch,
+        compiler_params=pltpu.CompilerParams(collective_id=1, has_side_effects=True, vmem_limit_bytes=48 << 20),
+    )(dense_re, dense_im, qt)
+
 
 def factor_inverse(diag):
     lane = lax.broadcasted_iota(jnp.int32, (NB, 4 * NB), 1)
@@ -40,50 +233,52 @@
     d = jnp.sum(jnp.where(lane == sub, w, 0.0), axis=1, keepdims=True)
     return w[:, 2 * NB :] * lax.rsqrt(d)
 
+
 def swapped(m):
     return jnp.concatenate([-m[:, NB:], m[:, :NB]], axis=1)
+
 
 def chol_kernel(scale, g_ref, y_ref, out_ref, a_ref):
     n = RANK
     rows = y_ref.shape[0]
     panels = n // NB
-    a_ref[:n, :] = g_ref[...]
-    a_ref[n:, :] = y_ref[...]
+    packed = g_ref[...]
+    turned = packed.T
+    sub = lax.broadcasted_iota(jnp.int32, (n, n), 0)
+    lane = lax.broadcasted_iota(jnp.int32, (n, n), 1)
+    g_re = jnp.where(sub >= lane, packed, turned)
+    g_im = jnp.where(sub > lane, -turned, jnp.where(sub == lane, 0.0, packed))
+    for k in range(panels):
+        a_ref[:n, 2 * NB * k : 2 * NB * k + NB] = g_re[:, NB * k : NB * k + NB]
+        a_ref[:n, 2 * NB * k + NB : 2 * NB * (k + 1)] = g_im[:, NB * k : NB * k + NB]
+        a_ref[n:, 2 * NB * k : 2 * NB * k + NB] = y_ref[:, NB * k : NB * k + NB]
+        a_ref[n:, 2 * NB * k + NB : 2 * NB * (k + 1)] = y_ref[:, n + NB * k : n + NB * k + NB]
     for k in range(panels):
         lo = k * NB
         inv = factor_inverse(a_ref[lo : lo + NB, 2 * lo : 2 * lo + 2 * NB])
         both = jnp.concatenate([inv, swapped(inv)], axis=0)
         ap = a_ref[lo + NB :, 2 * lo : 2 * lo + 2 * NB]
-        low = dott(ap, both)
-        x = low[low.shape[0] - rows :] * scale
-        out_ref[:, 0, lo : lo + NB] = x[:, :NB]
-        out_ref[:, 1, lo : lo + NB] = x[:, NB:]
+        low = dot_nt(ap, both, HI)
+        solved = low[low.shape[0] - rows :] * scale
+        out_ref[:, 0, lo : lo + NB] = solved[:, :NB]
+        out_ref[:, 1, lo : lo + NB] = solved[:, NB:]
         left = panels - 1 - k
         if left:
             lk = low[: left * NB]
-            sk = swapped(lk)
-            q = jnp.concatenate([lk.reshape(left, NB, 2 * NB), sk.reshape(left, NB, 2 * NB)], axis=1)
+            q = jnp.concatenate([lk.reshape(left, NB, 2 * NB), swapped(lk).reshape(left, NB, 2 * NB)], axis=1)
             q = q.reshape(left * 2 * NB, 2 * NB)
-            a_ref[lo + NB :, 2 * lo + 2 * NB :] -= dott(low, q)
+            a_ref[lo + NB :, 2 * lo + 2 * NB :] -= dot_nt(low, q, HI)
+
 
 def chol(g, y, scale):
+    vmem = pl.BlockSpec(memory_space=pltpu.VMEM)
     return pl.pallas_call(
         functools.partial(chol_kernel, scale),
         out_shape=jax.ShapeDtypeStruct((y.shape[0], 2, RANK), jnp.float32),
-        in_specs=[pl.BlockSpec(memory_space=pltpu.VMEM)] * 2,
-        out_specs=pl.BlockSpec(memory_space=pltpu.VMEM),
+        in_specs=[vmem] * 2,
+        out_specs=vmem,
         scratch_shapes=[pltpu.VMEM((RANK + y.shape[0], 2 * RANK), jnp.float32)],
     )(g, y)
-
-def interleave(re, im):
-    r = re.shape[0]
-    return jnp.stack([re.reshape(r, -1, NB), im.reshape(r, -1, NB)], axis=2).reshape(r, -1)
-
-
-def times_i(m):
-    r = m.shape[0]
-    pairs = m.reshape(r, -1, 2, NB)
-    return jnp.stack([-pairs[:, :, 1], pairs[:, :, 0]], axis=2).reshape(r, -1)
 
 
 def f32dot(a, b, dims, precision=None):
@@ -108,17 +303,9 @@
     sine = jnp.sin(ref_angle)
     dense_re = (outer_re * cosine + outer_im * sine).astype(jnp.bfloat16)
     dense_im = (outer_im * cosine - outer_re * sine).astype(jnp.bfloat16)
-    q1 = interleave(q_start[:, 0], q_start[:, 1])
-    q2 = interleave(q_start[:, 1], -q_start[:, 0])
-    adj = f32dot(dense_re, q1, ((0,), (0,))) + f32dot(dense_im, q2, ((0,), (0,)))
-    adj = lax.psum(adj, "row").astype(jnp.bfloat16)
-    image = f32dot(dense_re, adj, ((1,), (0,))) + f32dot(dense_im, times_i(adj), ((1,), (0,)))
-    image = lax.psum_scatter(image, "col", scatter_dimension=0, tiled=True)
-    im_re = image.reshape(-1, RANK // NB, 2, NB)[:, :, 0].reshape(-1, RANK)
-    im_im = image.reshape(-1, RANK // NB, 2, NB)[:, :, 1].reshape(-1, RANK)
-    gram = f32dot(im_re, image, ((0,), (0,)), HI) - f32dot(im_im, times_i(image), ((0,), (0,)), HI)
-    gram = lax.psum(gram, ("row", "col"))
-    return chol(gram, image, math.sqrt(NF))
+    qt = jnp.transpose(q_start, (1, 2, 0)).reshape(2 * RANK, -1)
+    image, gram = tail(dense_re, dense_im, qt)
+    return chol(gram.reshape(RANK, RANK), image, math.sqrt(NF))
 
 
 def solution(mesh):

time: 489 us -> 257 us (0.53)
  waiting for transfers between devices: 272 us -> 62.5 us
  blocking collectives: 110 us -> 58.9 us
  Pallas kernels: 31 us -> 80.9 us
  local copies, waits for them, and re-layouts: 26.7 us -> 17.2 us
  matrix products: 28.2 us -> 20.5 us
    psum x1 -> x0, waiting for transfers between devices: 147 us -> none  [body(): gram = lax.psum(gram, ('row', 'col'))]
    reduce_scatter x1 -> x0, waiting for transfers between devices: 73.5 us -> none  [body(): image = lax.psum_scatter(image, 'col', scatter_dimension=0, tiled=True)]
    psum x1 -> x0, blocking collectives: 51.1 us -> none  [body(): adj = lax.psum(adj, 'row').astype(jnp.bfloat16)]
    pallas_call x0 -> x1, Pallas kernels: none -> 49.4 us  [tail(): pl.pallas_call(tail_kernel, out_shape=(jax.ShapeDtypeStruct((64, 2 * RANK...]
    all_gather x1, waiting for transfers between devices: 51.5 us -> 62.5 us  [body(): piece = lax.all_gather(refl, 'col', axis=1, tiled=True)]
    dot_general x14 -> x8, matrix products: 27.3 us -> 19.6 us  [f32dot(): lax.dot_general(a, b, ((dims[0], dims[1]), ((), ())), precision=precision...]
    unnamed x23 -> x16, local copies, waits for them, and re-layouts: 9.53 us -> 3.3 us
  transfers between devices with their start and end apart: 3 -> 1, of which waited for: 3 -> 1; matrix products, arithmetic and copies ran while one was open for 4% -> 4% of each run, Pallas kernels for 0% -> 0%
where the time goes in v2:
time: 257 us
  Pallas kernels  80.9 us (31%)
  waiting for transfers between devices  62.5 us (24%)
  blocking collectives  58.9 us (23%)
  matrix products  20.5 us (8%)
  local copies, waits for them, and re-layouts  17.2 us (7%)
  between operations  13.5 us (5%)
  other arithmetic  3.1 us (1%)
    all_gather x1, waiting for transfers between devices, body(): piece = lax.all_gather(refl, 'col', axis=1, tiled=True)  62.5 us
    psum x1, blocking collectives, body(): lax.psum(jnp.stack([part_re, part_im]), 'row').astype(jnp.bfloat16)  58.9 us
    pallas_call x1, Pallas kernels, tail(): pl.pallas_call(tail_kernel, out_shape=(jax.ShapeDtypeStruct((64, 2 * RANK...  49.4 us
    pallas_call x1, Pallas kernels, chol(): pl.pallas_call(functools.partial(chol_kernel, scale), out_shape=jax.Shape...  31.4 us
    dot_general x8, matrix products, f32dot(): lax.dot_general(a, b, ((dims[0], dims[1]), ((), ())), precision=precision...  19.6 us
    cos x1, local copies, waits for them, and re-layouts, body(): cosine = jnp.cos(ref_angle)  9.42 us
  transfers between devices with their start and end apart: 1, of which 1 were waited for; matrix products, arithmetic and copies ran while one was open for 4% of the time, Pallas kernels for 0%

profile of v2, /device:TPU:0, one launch (start us, length us, event | category | flops | bytes accessed | tf_op | source)
XLA Modules:
  0.0 256.6 jit_solution(3817824294383680472)
XLA Ops:
  6.5 0.0 all-gather.2.cloned.1.call-start
  6.5 1.4 reshape.13
  8.0 0.7 add_select_fusion
  8.7 0.0 copy-start.4
  8.7 0.9 fusion.41
  9.6 0.4 copy.14
  10.0 1.2 reshape.14
  11.1 0.0 all-gather.2.cloned.1.call-update
  11.2 0.0 copy-done.4
  11.2 1.5 copy.19
  12.7 9.4 %fusion.44 = (f32[1024,512]{1,0:T(8,128)S(1)}, f32[1024,512]{1,0:T(8,128)}) fusion(f32[1024,512]{1,0:T(8,128)} %param.9), kind=kLoop, calls=%fused_computation.51 | loop fusion | bytes 6291456 | tf_op jit(solution)/shard_map/cos | solution.py:302
  22.1 62.5 %all-gather.2.cloned.1.call-done = bf16[2,1024,2048]{2,1,0:T(8,128)(2,1)} async-done(((bf16[2,64,2048]{2,1,0:T(8,128)(2,1)}), bf16[2,1024,2048]{2,1,0:T(8,128)(2,1)}) %all-gather.2.cloned.1.call-update) | async-done | bytes 8388624 | tf_op jit(solution)/shard_map/all_gather | solution.py:296
  84.6 0.0 copy-start.6
  84.6 0.0 copy-start.7
  84.6 5.3 %fusion.1 = f32[1024,512]{1,0:T(8,128)S(1)} fusion(bf16[2,1024,2048]{2,1,0:T(8,128)(2,1)} %all-gather.2.cloned.1.call-done, bf16[2,2048,512]{2,1,0:T(8,128)(2,1)} %param.7), kind=kOutput, calls=%fused_computation.5 | convolution fusion | flops 2147483648 | bytes 8388608 | tf_op jit(solution)/shard_map/dot_general | solution.py:285
  89.9 0.0 copy-done.6
  89.9 1.1 copy-done.7
  91.0 2.3 fusion.2
  93.3 2.3 add_bitcast_fusion
  95.7 2.3 subtract_bitcast_fusion
  98.0 2.4 pad_maximum_fusion
  100.4 58.9 %all-reduce.1 = bf16[2,1024,512]{2,1,0:T(8,128)(2,1)} all-reduce(f32[2,1024,512]{2,1,0:T(8,128)} %pad_maximum_fusion), channel_id=1, replica_groups=mesh['row'=8,'col'=16] {'row'}, use_global_device_ids=true, to_apply=%region_0.1 | all-reduce | flops 1048576 | bytes 6291456 | tf_op jit(solution)/shard_map/psum | solution.py:299
  159.3 0.0 copy-start.3
  159.3 0.0 copy-start.5
  159.3 3.2 %fusion.9 = f32[512,1024]{0,1:T(8,128)S(1)} fusion(bf16[2,1024,1024]{2,1,0:T(8,128)(2,1)} %param.8, bf16[2,1024,512]{2,1,0:T(8,128)(2,1)} %all-reduce.1), kind=kOutput, calls=%fused_computation.17 | convolution fusion | flops 1073741824 | bytes 5242880 | tf_op jit(solution)/shard_map/dot_general | solution.py:285
  162.5 0.0 copy-done.3
  162.5 0.5 copy-done.5
  163.0 1.3 fusion.11
  164.3 0.0 copy-start.2
  164.3 1.2 fusion.37
  165.6 0.3 copy-done.2
  165.9 1.6 fusion.8
  167.5 49.4 %shard_map.64 = (f32[64,512]{1,0:T(8,128)S(1)}, f32[16,16,256]{2,1,0:T(8,128)S(1)}) custom-call(bf16[1024,512]{1,0:T(8,128)(2,1)S(1)} %get-tuple-element.10.dense_re, bf16[1024,512]{1,0:T(8,128)(2,1)S(1)} %get-tuple-element.9.dense_im, bf16[512,1024]{1,0:T(8,128)(2,1)S(1)} %bitcast.79), custom_call_target="tpu_custom_call" | custom-call | tf_op jit(solution)/shard_map/pallas_call | solution.py:203
  216.9 0.0 copy-start
  216.9 0.7 copy-done
  217.6 0.0 copy-start.1
  217.6 0.6 copy-done.1
  218.3 31.4 %shard_map.65 = f32[64,2,256]{2,1,0:T(2,128)} custom-call(f32[256,256]{1,0:T(8,128)} %bitcast.80, f32[64,512]{1,0:T(8,128)} %copy-done.1), custom_call_target="tpu_custom_call" | custom-call | tf_op jit(solution)/shard_map/pallas_call | solution.py:275
  (1 shorter events, 0.0 us)
Async XLA Ops:
  6.5 78.0 %all-gather.2.cloned.1.call-start = ((), (), s32[]{:S(2)}) async-start(), calls=%async_computation | async-start | bytes 8912896 | tf_op jit(solution)/shard_map/all_gather | solution.py:296
  8.7 2.5 copy-start.4
  84.6 5.3 %copy-start.6 = (bf16[2,1024,2048]{2,1,0:T(8,128)(2,1)S(1)}, bf16[2,1024,2048]{2,1,0:T(8,128)(2,1)}, u32[]{:S(2)}) copy-start(bf16[2,1024,2048]{2,1,0:T(8,128)(2,1)} %all-gather.2.cloned.1.call-done) | copy-start | bytes 25165828
  84.6 6.4 %copy-start.7 = (bf16[2,2048,512]{2,1,0:T(8,128)(2,1)S(1)}, bf16[2,2048,512]{2,1,0:T(8,128)(2,1)}, u32[]{:S(2)}) copy-start(bf16[2,2048,512]{2,1,0:T(8,128)(2,1)} %param.7) | copy-start | bytes 12582916
  159.3 3.3 %copy-start.3 = (bf16[2,1024,512]{2,1,0:T(8,128)(2,1)S(1)}, bf16[2,1024,512]{2,1,0:T(8,128)(2,1)}, u32[]{:S(2)}) copy-start(bf16[2,1024,512]{2,1,0:T(8,128)(2,1)} %all-reduce.1) | copy-start | bytes 6291460
  159.3 3.8 %copy-start.5 = (bf16[2,1024,1024]{2,1,0:T(8,128)(2,1)S(1)}, bf16[2,1024,1024]{2,1,0:T(8,128)(2,1)}, u32[]{:S(2)}) copy-start(bf16[2,1024,1024]{2,1,0:T(8,128)(2,1)} %param.8) | copy-start | bytes 12582916
  164.3 1.6 copy-start.2
  216.9 0.7 copy-start
  217.6 0.6 copy-start.1
Sparse Core Ops, SparseCore 0:
  11.3 73.2 all-gather.1

commit v3 on v2

--- a/solution.py
+++ b/solution.py
@@ -32,6 +32,256 @@
     return pltpu.make_async_remote_copy(
         src_ref=src, dst_ref=dst, send_sem=send_sem, recv_sem=recv_sem, device_id=(row, col), device_id_type=MESH
     )
+
+
+def cos_sin(angle):
+    half = 0.5 * angle
+    t = half * half
+    s = -1.0 / 39916800.0
+    for k in (1.0 / 362880.0, -1.0 / 5040.0, 1.0 / 120.0, -1.0 / 6.0, 1.0):
+        s = s * t + k
+    s = s * half
+    c = 1.0 / 479001600.0
+    for k in (-1.0 / 3628800.0, 1.0 / 40320.0, -1.0 / 720.0, 1.0 / 24.0, -0.5, 1.0):
+        c = c * t + k
+    return 1.0 - 2.0 * s * s, 2.0 * s * c
+
+
+def head_kernel(
+    refl_ref, order_ref, focus_in_hbm, focus_out_hbm, angle_hbm, dense_re, dense_im,
+    gat, p_ref, f_ref, angle, cpart, crecv, zsend, zrecv, cfull,
+    local_sem, gs, gr, ps, pr, zs, zr, cs, cr, ws, wr,
+):
+    r = lax.axis_index("row")
+    c = lax.axis_index("col")
+    z, core = r // 2, r % 2
+    x, y = c // 4, c % 4
+    other = 1 - core
+    up = {"x": (x + 1) % 4, "y": (y + 1) % 4}
+    down = {"x": (x + 3) % 4, "y": (y + 3) % 4}
+    far_x, far_y = (x + 2) % 4, (y + 2) % 4
+    left, right, low, high = down["x"], up["x"], down["y"], up["y"]
+
+    loads = [
+        pltpu.make_async_copy(focus_in_hbm, p_ref, local_sem.at[0]),
+        pltpu.make_async_copy(focus_out_hbm, f_ref, local_sem.at[1]),
+        pltpu.make_async_copy(angle_hbm, angle, local_sem.at[2]),
+    ]
+    for copy in loads:
+        copy.start()
+    barrier = pltpu.get_barrier_semaphore()
+    for to in ((r, right * 4 + y), (r, left * 4 + y), (r, x * 4 + high), (r, x * 4 + low), (z * 2 + other, c)):
+        pl.semaphore_signal(barrier, inc=1, device_id=to, device_id_type=MESH)
+    for d in range(1, 4):
+        pl.semaphore_signal(barrier, inc=1, device_id=((z + d) % 4 * 2 + core, c), device_id_type=MESH)
+
+    sub = lax.broadcasted_iota(jnp.int32, (PANEL_W, PANEL_W), 0)
+    for b in range(refl_ref.shape[2] // PANEL_W):
+        lanes = pl.ds(b * PANEL_W, PANEL_W)
+        place = order_ref[:, lanes] & (PANEL_W - 1)
+        onehot = jnp.where(place == sub, 1.0, 0.0).astype(jnp.bfloat16)
+        raw = jnp.concatenate([refl_ref[0, :32, lanes], refl_ref[1, :32, lanes], refl_ref[0, 32:, lanes], refl_ref[1, 32:, lanes]], axis=0)
+        moved = dot_nt(raw, onehot).astype(jnp.bfloat16)
+        gat[x, y, 0, :, lanes] = moved[:64]
+        gat[x, y, 1, :, lanes] = moved[64:]
+    pl.semaphore_wait(barrier, 8)
+
+    copies = {}
+
+    def send(name, sx, sy, h, piece=None):
+        axis, way = name[-2], name[-1]
+        to = (up if way == "+" else down)[axis]
+        col = to * 4 + y if axis == "x" else x * 4 + to
+        ref = gat.at[sx, sy, h] if piece is None else gat.at[sx, sy, h, pl.ds(32 * piece, 32)]
+        i = len(copies)
+        copies[name] = remote(ref, ref, gs.at[i], gr.at[i], r, col)
+        copies[name].start()
+
+    def got(*names):
+        for name in names:
+            copies[name + "+"].wait_recv()
+            copies[name + "-"].wait_recv()
+
+    def both(name, sx, sy, h):
+        send(name + "+", sx, sy, h)
+        send(name + "-", sx, sy, h)
+
+    def gemm(s, parts):
+        @pl.loop(0, 2)
+        def _(n):
+            lanes = pl.ds(pl.multiple_of(n * 256, 256), 256)
+            rows = jnp.concatenate([gat[sx, sy, h] for sx, sy, h in parts], axis=0)
+            by_re = dot_nn(rows, p_ref[0, :, lanes]).reshape(4, 2, 32, 256)
+            by_im = dot_nn(rows, p_ref[1, :, lanes]).reshape(4, 2, 32, 256)
+            cpart[s, 0, :, :, lanes] = by_re[:, 0] - by_im[:, 1]
+            cpart[s, 1, :, :, lanes] = by_im[:, 0] + by_re[:, 1]
+
+    pair, across, back, relay = {}, {}, {}, {}
+
+    def start_pair(s):
+        pair[s] = remote(cpart.at[s, other], crecv.at[s], ps.at[s], pr.at[s], z * 2 + other, c)
+        pair[s].start()
+
+    def start_across(s):
+        pair[s].wait_recv()
+        zsend[s] = cpart[s, core] + crecv[s]
+        across[s] = []
+        for d in range(1, 4):
+            to = (z + d) % 4
+            across[s].append(remote(zsend.at[s, to], zrecv.at[s, d - 1], zs.at[s, d - 1], zr.at[s, d - 1], to * 2 + core, c))
+            across[s][-1].start()
+
+    def place_of(parts, q):
+        first = jnp.int32(0)
+        for i, (sx, sy, h) in enumerate(parts):
+            first = first + jnp.where(q == i, 1, 0) * (sx * 256 + sy * 64 + h * 32)
+        return pl.multiple_of(first, 32)
+
+    def start_back(s, parts):
+        total = zsend[s, z]
+        for d in range(1, 4):
+            across[s][d - 1].wait_recv()
+            total = total + zrecv[s, d - 1]
+        mine = pl.ds(place_of(parts, z), 32)
+        cfull[core, mine, :] = total.astype(jnp.bfloat16)
+        ref = cfull.at[core, mine, :]
+        back[s] = []
+        for d in range(1, 4):
+            back[s].append(remote(ref, ref, cs.at[s, d - 1], cr.at[s, d - 1], (z + d) % 4 * 2 + core, c))
+            back[s][-1].start()
+        relay[s] = [remote(ref, ref, ws.at[s, 0], wr.at[s, 0], z * 2 + other, c)]
+        relay[s][0].start()
+
+    def start_relay(s, parts):
+        for d in range(1, 4):
+            back[s][d - 1].wait_recv()
+            ref = cfull.at[core, pl.ds(place_of(parts, (z + 4 - d) % 4), 32), :]
+            relay[s].append(remote(ref, ref, ws.at[s, d], wr.at[s, d], z * 2 + other, c))
+            relay[s][-1].start()
+
+    def finish(s):
+        for copy in relay[s]:
+            copy.wait_recv()
+
+    batches = [
+        [(x, y, 0), (x, y, 1), (left, y, 0), (right, y, 0)],
+        [(x, low, 1), (x, high, 1), (x, low, 0), (x, high, 0)],
+        [(left, y, 1), (right, y, 1), (x, far_y, 1), (far_x, y, 0)],
+        [(left, low, 0), (left, high, 0), (left, low, 1), (right, low, 1)],
+        [(right, low, 0), (right, high, 0), (left, high, 1), (right, high, 1)],
+        [(x, far_y, 0), (far_x, y, 1), (far_x, low, 0), (far_x, high, 0)],
+        [(left, far_y, 1), (right, far_y, 1), (left, far_y, 0), (far_x, low, 1)],
+        [(right, far_y, 0), (far_x, high, 1), (far_x, far_y, 0), (far_x, far_y, 1)],
+    ]
+
+    def progress(s):
+        if 0 <= s - 1 < 8:
+            start_across(s - 1)
+        if 0 <= s - 2 < 8:
+            start_back(s - 2, batches[s - 2])
+        if 0 <= s - 3 < 8:
+            start_relay(s - 3, batches[s - 3])
+        if 0 <= s - 4 < 8:
+            finish(s - 4)
+
+    both("Ax", x, y, 0)
+    both("By", x, y, 1)
+    both("Ay", x, y, 0)
+    both("Bx", x, y, 1)
+    loads[0].wait()
+    for s in range(8):
+        if s == 0:
+            got("Ax")
+            send("Aqx+", left, y, 0, 0)
+            send("Aqx-", right, y, 0, 1)
+            got("By")
+            send("Bqy+", x, low, 1, 0)
+            send("Bqy-", x, high, 1, 1)
+            both("A1y", left, y, 0)
+            both("B1x", x, low, 1)
+            both("A2y", right, y, 0)
+            both("B2x", x, high, 1)
+        elif s == 1:
+            got("Ay")
+            send("Aq0y+", x, low, 0, 0)
+            send("Aq0y-", x, high, 0, 1)
+            got("Bx")
+            send("Bq0x+", left, y, 1, 0)
+            send("Bq0x-", right, y, 1, 1)
+        elif s == 2:
+            got("Aqx")
+            both("A3y", far_x, y, 0)
+            got("Bqy")
+            both("B3x", x, far_y, 1)
+        elif s == 3:
+            got("A1y")
+            send("Aq1y+", left, low, 0, 0)
+            send("Aq1y-", left, high, 0, 1)
+            got("B1x")
+            send("Bq1x+", left, low, 1, 0)
+            send("Bq1x-", right, low, 1, 1)
+        elif s == 4:
+            got("A2y")
+            send("Aq2y+", right, low, 0, 0)
+            send("Aq2y-", right, high, 0, 1)
+            got("B2x")
+            send("Bq2x+", left, high, 1, 0)
+            send("Bq2x-", right, high, 1, 1)
+        elif s == 5:
+            got("Aq0y", "Bq0x", "A3y")
+            send("Aq3y+", far_x, low, 0, 0)
+            send("Aq3y-", far_x, high, 0, 1)
+            got("B3x")
+            send("Bq3x+", left, far_y, 1, 0)
+            send("Bq3x-", right, far_y, 1, 1)
+        elif s == 6:
+            got("Aq1y", "Bq1x")
+        else:
+            got("Aq2y", "Bq2x", "Aq3y", "Bq3x")
+        progress(s)
+        gemm(s, batches[s])
+        start_pair(s)
+    for s in range(8, 12):
+        progress(s)
+
+    loads[1].wait()
+    loads[2].wait()
+
+    @pl.loop(0, 8)
+    def _(m):
+        rows = pl.ds(pl.multiple_of(m * 128, 128), 128)
+        f_re, f_im = f_ref[0, rows, :], f_ref[1, rows, :]
+        outer_re = dot_nn(f_re, cfull[0]) - dot_nn(f_im, cfull[1])
+        outer_im = dot_nn(f_re, cfull[1]) + dot_nn(f_im, cfull[0])
+        cosine, sine = cos_sin(angle[rows, :])
+        dense_re[rows, :] = (outer_re * cosine + outer_im * sine).astype(jnp.bfloat16)
+        dense_im[rows, :] = (outer_im * cosine - outer_re * sine).astype(jnp.bfloat16)
+
+    for copy in list(copies.values()) + [pair[s] for s in range(8)]:
+        copy.wait_send()
+    for s in range(8):
+        for copy in across[s] + back[s] + relay[s]:
+            copy.wait_send()
+
+
+def head(reflection, order, focus_in, focus_out, ref_angle):
+    bf, f32 = jnp.bfloat16, jnp.float32
+    vm, dma = pltpu.VMEM, pltpu.SemaphoreType.DMA
+    vmem = pl.BlockSpec(memory_space=pltpu.VMEM)
+    anywhere = pl.BlockSpec(memory_space=pl.ANY)
+    scratch = [
+        vm((4, 4, 2, 64, 2048), bf), vm((2, 2048, 512), bf), vm((2, 1024, 1024), bf), vm((1024, 512), f32),
+        vm((8, 2, 4, 32, 512), f32), vm((8, 4, 32, 512), f32), vm((8, 4, 32, 512), f32), vm((8, 3, 32, 512), f32), vm((2, 1024, 512), bf),
+        dma((3,)), dma((40,)), dma((40,)), dma((8,)), dma((8,)), dma((8, 3)), dma((8, 3)), dma((8, 3)), dma((8, 3)), dma((8, 4)), dma((8, 4)),
+    ]
+    return pl.pallas_call(
+        head_kernel,
+        out_shape=(jax.ShapeDtypeStruct((1024, 512), bf), jax.ShapeDtypeStruct((1024, 512), bf)),
+        in_specs=[vmem, vmem, anywhere, anywhere, anywhere],
+        out_specs=(vmem, vmem),
+        scratch_shapes=scratch,
+        compiler_params=pltpu.CompilerParams(collective_id=0, has_side_effects=True, vmem_limit_bytes=56 << 20),
+    )(reflection, order, focus_in, focus_out, ref_angle)
 
 
 def tail_kernel(
@@ -281,28 +531,8 @@
     )(g, y)
 
 
-def f32dot(a, b, dims, precision=None):
-    return lax.dot_general(a, b, ((dims[0], dims[1]), ((), ())), precision=precision, preferred_element_type=jnp.float32)
-
-
 def body(reflection, focus_in, focus_out, ref_angle, element_order, q_start):
-    local_inputs = focus_in.shape[1]
-    blocks = local_inputs // PANEL_W
-    place = (element_order % PANEL_W).reshape(blocks, PANEL_W)
-    onehot = (place[:, :, None] == jnp.arange(PANEL_W, dtype=jnp.int32)).astype(jnp.bfloat16)
-    refl = reflection.reshape(2 * reflection.shape[1], blocks, PANEL_W)
-    refl = jnp.einsum("mbt,bts->mbs", refl, onehot, preferred_element_type=jnp.float32).astype(jnp.bfloat16)
-    refl = refl.reshape(reflection.shape)
-    piece = lax.all_gather(refl, "col", axis=1, tiled=True)
-    part_re = f32dot(piece[0], focus_in[0], ((1,), (0,))) - f32dot(piece[1], focus_in[1], ((1,), (0,)))
-    part_im = f32dot(piece[0], focus_in[1], ((1,), (0,))) + f32dot(piece[1], focus_in[0], ((1,), (0,)))
-    focused = lax.psum(jnp.stack([part_re, part_im]), "row").astype(jnp.bfloat16)
-    outer_re = f32dot(focus_out[0], focused[0], ((1,), (0,))) - f32dot(focus_out[1], focused[1], ((1,), (0,)))
-    outer_im = f32dot(focus_out[0], focused[1], ((1,), (0,))) + f32dot(focus_out[1], focused[0], ((1,), (0,)))
-    cosine = jnp.cos(ref_angle)
-    sine = jnp.sin(ref_angle)
-    dense_re = (outer_re * cosine + outer_im * sine).astype(jnp.bfloat16)
-    dense_im = (outer_im * cosine - outer_re * sine).astype(jnp.bfloat16)
+    dense_re, dense_im = head(reflection, element_order.reshape(1, -1), focus_in, focus_out, ref_angle)
     qt = jnp.transpose(q_start, (1, 2, 0)).reshape(2 * RANK, -1)
     image, gram = tail(dense_re, dense_im, qt)
     return chol(gram.reshape(RANK, RANK), image, math.sqrt(NF))

time: 257 us -> 165 us (0.64)
  Pallas kernels: 80.9 us -> 159 us
  waiting for transfers between devices: 62.5 us -> 0 us
  blocking collectives: 58.9 us -> 0 us
  matrix products: 20.5 us -> 0 us
  between operations: 13.5 us -> 0.04 us
  local copies, waits for them, and re-layouts: 17.2 us -> 6.22 us
  other arithmetic: 3.1 us -> 0 us
    pallas_call x0 -> x1, Pallas kernels: none -> 77.3 us  [head(): pl.pallas_call(head_kernel, out_shape=(jax.ShapeDtypeStruct((1024, 512),...]
    all_gather x1 -> x0, waiting for transfers between devices: 62.5 us -> none  [body(): piece = lax.all_gather(refl, 'col', axis=1, tiled=True)]
    psum x1 -> x0, blocking collectives: 58.9 us -> none  [body(): lax.psum(jnp.stack([part_re, part_im]), 'row').astype(jnp.bfloat16)]
    dot_general x9 -> x0, matrix products: 20.5 us -> none  [the longest x8 19.6 us: f32dot(): lax.dot_general(a, b, ((dims[0], dims[1]), ((), ())), precision=precision...]
    cos x1 -> x0, local copies, waits for them, and re-layouts: 9.42 us -> none  [body(): cosine = jnp.cos(ref_angle)]
    reshape x2 -> x0, local copies, waits for them, and re-layouts: 2.61 us -> none  [the longest x1 1.43 us: body(): refl = reflection.reshape(2 * reflection.shape[1], blocks, PANEL_W)]
  transfers between devices with their start and end apart: 1 -> 0, of which waited for: 1 -> 0; matrix products, arithmetic and copies ran while one was open for 4% -> 0% of each run, Pallas kernels for 0% -> 0%
where the time goes in v3:
time: 165 us
  Pallas kernels  159 us (96%)
  local copies, waits for them, and re-layouts  6.22 us (4%)
    pallas_call x1, Pallas kernels, head(): pl.pallas_call(head_kernel, out_shape=(jax.ShapeDtypeStruct((1024, 512),...  77.3 us
    pallas_call x1, Pallas kernels, tail(): pl.pallas_call(tail_kernel, out_shape=(jax.ShapeDtypeStruct((64, 2 * RANK...  50.2 us
    pallas_call x1, Pallas kernels, chol(): pl.pallas_call(functools.partial(chol_kernel, scale), out_shape=jax.Shape...  31.2 us
    unnamed x8, local copies, waits for them, and re-layouts  3.78 us

profile of v3, /device:TPU:0, one launch (start us, length us, event | category | flops | bytes accessed | tf_op | source)
XLA Modules:
  0.0 165.0 jit_solution(3563266814264888230)
XLA Ops:
  0.0 2.4 %copy.7 = bf16[2,256,1024]{2,1,0:T(8,128)(2,1)S(1)} copy(bf16[2,256,1024]{1,0,2:T(2,128)(2,1)} %bitcast.6) | data formatting | bytes 2097152 | tf_op jit(solution)/shard_map/transpose | solution.py:536
  2.5 77.3 %shard_map.64 = (bf16[1024,512]{1,0:T(8,128)(2,1)}, bf16[1024,512]{1,0:T(8,128)(2,1)}) custom-call(bf16[2,64,2048]{2,1,0:T(8,128)(2,1)} %refl_ref.1, s32[1,2048]{1,0:T(1,128)} %bitcast.7, bf16[2,2048,512]{2,1,0:T(8,128)(2,1)} %focus_in_hbm.1, bf16[2,1024,1024]{2,1,0:T(8,128)(2,1)} %focus_out_hbm.1, f32[1024,512]{1,0:T(8,128)} %angle_hbm.1), custom_call_target="tpu_custom_call" | custom-call | tf_op jit(solution)/shard_map/pallas_call | solution.py:277
  79.8 0.0 copy-start
  79.8 1.2 copy-done
  81.0 0.0 copy-start.1
  81.0 1.2 copy-done.1
  82.2 50.2 %shard_map.65 = (f32[64,512]{1,0:T(8,128)S(1)}, f32[16,16,256]{2,1,0:T(8,128)S(1)}) custom-call(bf16[1024,512]{1,0:T(8,128)(2,1)S(1)} %copy-done, bf16[1024,512]{1,0:T(8,128)(2,1)S(1)} %copy-done.1, bf16[512,1024]{1,0:T(8,128)(2,1)S(1)} %bitcast.4), custom_call_target="tpu_custom_call" | custom-call | tf_op jit(solution)/shard_map/pallas_call | solution.py:453
  132.4 0.0 copy-start.2
  132.4 0.7 copy-done.2
  133.1 0.0 copy-start.3
  133.1 0.6 copy-done.3
  133.8 31.2 %shard_map.66 = f32[64,2,256]{2,1,0:T(2,128)} custom-call(f32[256,256]{1,0:T(8,128)} %bitcast.5, f32[64,512]{1,0:T(8,128)} %copy-done.3), custom_call_target="tpu_custom_call" | custom-call | tf_op jit(solution)/shard_map/pallas_call | solution.py:525
Async XLA Ops:
  79.8 1.2 copy-start
  81.0 1.2 copy-start.1
  132.4 0.7 copy-start.2
  133.1 0.6 copy-start.3

commit v4 on v3

--- a/solution.py
+++ b/solution.py
@@ -47,10 +47,14 @@
     return 1.0 - 2.0 * s * s, 2.0 * s * c
 
 
-def head_kernel(
-    refl_ref, order_ref, focus_in_hbm, focus_out_hbm, angle_hbm, dense_re, dense_im,
-    gat, p_ref, f_ref, angle, cpart, crecv, zsend, zrecv, cfull,
+def front_kernel(
+    refl_ref, order_ref, q_ref, focus_in_hbm, focus_out_hbm, angle_hbm, image_ref, gram_ref,
+    gat, p_ref, f_ref, cosine, sine, cpart, crecv, zsend, zrecv, cfull, last_pair, last_recv, last_send, last_across, acc, dense_re, dense_im,
+    qt, zown, zs1, zr1, zs2, zr2, zfull,
+    yown_a, yown_b, ysa, ysb, yra, yrb, ys2, yr2a, yr2b,
+    hpart, hrecv, hrow,
     local_sem, gs, gr, ps, pr, zs, zr, cs, cr, ws, wr,
+    sz1, rz1, sz2, rz2, sz3, rz3, sz4, rz4, sya, rya, syb, ryb, sy2a, ry2a, sy2b, ry2b, sh1, rh1, sh2, rh2, sh3, rh3,
 ):
     r = lax.axis_index("row")
     c = lax.axis_index("col")
@@ -65,15 +69,15 @@
     loads = [
         pltpu.make_async_copy(focus_in_hbm, p_ref, local_sem.at[0]),
         pltpu.make_async_copy(focus_out_hbm, f_ref, local_sem.at[1]),
-        pltpu.make_async_copy(angle_hbm, angle, local_sem.at[2]),
+        pltpu.make_async_copy(angle_hbm, cosine, local_sem.at[2]),
     ]
     for copy in loads:
         copy.start()
     barrier = pltpu.get_barrier_semaphore()
-    for to in ((r, right * 4 + y), (r, left * 4 + y), (r, x * 4 + high), (r, x * 4 + low), (z * 2 + other, c)):
-        pl.semaphore_signal(barrier, inc=1, device_id=to, device_id_type=MESH)
-    for d in range(1, 4):
-        pl.semaphore_signal(barrier, inc=1, device_id=((z + d) % 4 * 2 + core, c), device_id_type=MESH)
+    for d in range(1, 8):
+        pl.semaphore_signal(barrier, inc=1, device_id=((r + d) % 8, c), device_id_type=MESH)
+    for d in range(1, 16):
+        pl.semaphore_signal(barrier, inc=1, device_id=(r, (c + d) % 16), device_id_type=MESH)
 
     sub = lax.broadcasted_iota(jnp.int32, (PANEL_W, PANEL_W), 0)
     for b in range(refl_ref.shape[2] // PANEL_W):
@@ -84,7 +88,7 @@
         moved = dot_nt(raw, onehot).astype(jnp.bfloat16)
         gat[x, y, 0, :, lanes] = moved[:64]
         gat[x, y, 1, :, lanes] = moved[64:]
-    pl.semaphore_wait(barrier, 8)
+    pl.semaphore_wait(barrier, 22)
 
     copies = {}
 
@@ -119,16 +123,29 @@
     pair, across, back, relay = {}, {}, {}, {}
 
     def start_pair(s):
-        pair[s] = remote(cpart.at[s, other], crecv.at[s], ps.at[s], pr.at[s], z * 2 + other, c)
+        if s == 7:
+            last_pair[...] = cpart[s, other].astype(jnp.bfloat16)
+            pair[s] = remote(last_pair, last_recv, ps.at[s], pr.at[s], z * 2 + other, c)
+        else:
+            pair[s] = remote(cpart.at[s, other], crecv.at[s], ps.at[s], pr.at[s], z * 2 + other, c)
         pair[s].start()
 
     def start_across(s):
         pair[s].wait_recv()
-        zsend[s] = cpart[s, core] + crecv[s]
         across[s] = []
+        if s == 7:
+            mine = cpart[s, core] + last_recv[...].astype(jnp.float32)
+            last_send[...] = mine.astype(jnp.bfloat16)
+        else:
+            mine = cpart[s, core] + crecv[s]
+        zsend[s] = mine
         for d in range(1, 4):
             to = (z + d) % 4
-            across[s].append(remote(zsend.at[s, to], zrecv.at[s, d - 1], zs.at[s, d - 1], zr.at[s, d - 1], to * 2 + core, c))
+            if s == 7:
+                src, dst = last_send.at[to], last_across.at[d - 1]
+            else:
+                src, dst = zsend.at[s, to], zrecv.at[s, d - 1]
+            across[s].append(remote(src, dst, zs.at[s, d - 1], zr.at[s, d - 1], to * 2 + core, c))
             across[s][-1].start()
 
     def place_of(parts, q):
@@ -141,7 +158,7 @@
         total = zsend[s, z]
         for d in range(1, 4):
             across[s][d - 1].wait_recv()
-            total = total + zrecv[s, d - 1]
+            total = total + (last_across[d - 1].astype(jnp.float32) if s == 7 else zrecv[s, d - 1])
         mine = pl.ds(place_of(parts, z), 32)
         cfull[core, mine, :] = total.astype(jnp.bfloat16)
         ref = cfull.at[core, mine, :]
@@ -241,87 +258,79 @@
         progress(s)
         gemm(s, batches[s])
         start_pair(s)
-    for s in range(8, 12):
-        progress(s)
-
+        if s == 2:
+            loads[2].wait()
+
+            @pl.loop(0, 8)
+            def _(m):
+                rows = pl.ds(pl.multiple_of(m * 128, 128), 128)
+                cosine[rows, :], sine[rows, :] = cos_sin(cosine[rows, :])
+        if s == 3:
+            qt[0] = q_ref[:, 0, :].T
+            qt[1] = q_ref[:, 1, :].T
+
+    def outer(to, rows):
+        lanes = pl.ds(pl.multiple_of(to * 256, 256), 256)
+        f_re, f_im = f_ref[0, rows, lanes], f_ref[1, rows, lanes]
+        c_re, c_im = cfull[0, lanes, :], cfull[1, lanes, :]
+        return dot_nn(f_re, c_re) - dot_nn(f_im, c_im), dot_nn(f_re, c_im) + dot_nn(f_im, c_re)
+
+    progress(8)
+    finish(5)
     loads[1].wait()
-    loads[2].wait()
 
     @pl.loop(0, 8)
     def _(m):
         rows = pl.ds(pl.multiple_of(m * 128, 128), 128)
-        f_re, f_im = f_ref[0, rows, :], f_ref[1, rows, :]
-        outer_re = dot_nn(f_re, cfull[0]) - dot_nn(f_im, cfull[1])
-        outer_im = dot_nn(f_re, cfull[1]) + dot_nn(f_im, cfull[0])
-        cosine, sine = cos_sin(angle[rows, :])
-        dense_re[rows, :] = (outer_re * cosine + outer_im * sine).astype(jnp.bfloat16)
-        dense_im[rows, :] = (outer_im * cosine - outer_re * sine).astype(jnp.bfloat16)
-
-    for copy in list(copies.values()) + [pair[s] for s in range(8)]:
-        copy.wait_send()
-    for s in range(8):
-        for copy in across[s] + back[s] + relay[s]:
-            copy.wait_send()
-
-
-def head(reflection, order, focus_in, focus_out, ref_angle):
-    bf, f32 = jnp.bfloat16, jnp.float32
-    vm, dma = pltpu.VMEM, pltpu.SemaphoreType.DMA
-    vmem = pl.BlockSpec(memory_space=pltpu.VMEM)
-    anywhere = pl.BlockSpec(memory_space=pl.ANY)
-    scratch = [
-        vm((4, 4, 2, 64, 2048), bf), vm((2, 2048, 512), bf), vm((2, 1024, 1024), bf), vm((1024, 512), f32),
-        vm((8, 2, 4, 32, 512), f32), vm((8, 4, 32, 512), f32), vm((8, 4, 32, 512), f32), vm((8, 3, 32, 512), f32), vm((2, 1024, 512), bf),
-        dma((3,)), dma((40,)), dma((40,)), dma((8,)), dma((8,)), dma((8, 3)), dma((8, 3)), dma((8, 3)), dma((8, 3)), dma((8, 4)), dma((8, 4)),
-    ]
-    return pl.pallas_call(
-        head_kernel,
-        out_shape=(jax.ShapeDtypeStruct((1024, 512), bf), jax.ShapeDtypeStruct((1024, 512), bf)),
-        in_specs=[vmem, vmem, anywhere, anywhere, anywhere],
-        out_specs=(vmem, vmem),
-        scratch_shapes=scratch,
-        compiler_params=pltpu.CompilerParams(collective_id=0, has_side_effects=True, vmem_limit_bytes=56 << 20),
-    )(reflection, order, focus_in, focus_out, ref_angle)
-
-
-def tail_kernel(
-    dense_re, dense_im, qt_ref, image_ref, gram_ref,
-    zpart, zs1, zr1, zs2, zr2, zfull,
-    yown_a, yown_b, ysa, ysb, yra, yrb, ys2, yr2a, yr2b,
-    hpart, hrecv, hrow,
-    sz1, rz1, sz2, rz2, sz3, rz3, sz4, rz4, sya, rya, syb, ryb, sy2a, ry2a, sy2b, ry2b, sh1, rh1, sh2, rh2, sh3, rh3,
-):
-    r = lax.axis_index("row")
-    c = lax.axis_index("col")
-    z, core = r // 2, r % 2
-    x, y = c // 4, c % 4
-    other = 1 - core
-
-    barrier = pltpu.get_barrier_semaphore()
-    for d in range(1, 8):
-        pl.semaphore_signal(barrier, inc=1, device_id=((r + d) % 8, c), device_id_type=MESH)
-    for d in range(1, 16):
-        pl.semaphore_signal(barrier, inc=1, device_id=(r, (c + d) % 16), device_id_type=MESH)
+        acc[0, rows, :], acc[1, rows, :] = outer(x, rows)
+
+    start_back(7, batches[7])
+    start_relay(6, batches[6])
+    finish(6)
+
+    @pl.loop(0, 8)
+    def _(m):
+        rows = pl.ds(pl.multiple_of(m * 128, 128), 128)
+        add_re, add_im = outer(left, rows)
+        acc[0, rows, :] += add_re
+        acc[1, rows, :] += add_im
+
+    start_relay(7, batches[7])
+    finish(7)
+
+    @pl.loop(0, 8)
+    def _(m):
+        rows = pl.ds(pl.multiple_of(m * 128, 128), 128)
+        right_re, right_im = outer(right, rows)
+        far_re, far_im = outer(far_x, rows)
+        outer_re = acc[0, rows, :] + (right_re + far_re)
+        outer_im = acc[1, rows, :] + (right_im + far_im)
+        co, si = cosine[rows, :], sine[rows, :]
+        dense_re[rows, :] = (outer_re * co + outer_im * si).astype(jnp.bfloat16)
+        dense_im[rows, :] = (outer_im * co - outer_re * si).astype(jnp.bfloat16)
+
 
     half = RANK
-    q1 = qt_ref[...]
-    q2 = jnp.concatenate([q1[half:], -q1[:half]], axis=0)
-    zpart[...] = dot_nn(q1, dense_re[...]) + dot_nn(q2, dense_im[...])
-    pl.semaphore_wait(barrier, 22)
-    zs1[...] = zpart[pl.ds(other * half, half), :].astype(zs1.dtype)
-    pair = remote(zs1, zr1, sz1, rz1, z * 2 + other, c)
-    pair.start()
-    pair.wait_recv()
-    mine = zpart[pl.ds(core * half, half), :] + zr1[...].astype(jnp.float32)
+
+    def z_half(h, sign):
+        return dot_nn(qt[h], dense_re[...]) + sign * dot_nn(qt[1 - h], dense_im[...])
+
+    sign = (1 - 2 * core).astype(jnp.float32)
+    zs1[...] = z_half(other, -sign).astype(jnp.bfloat16)
+    swap = remote(zs1, zr1, sz1, rz1, z * 2 + other, c)
+    swap.start()
+    zown[...] = z_half(core, sign)
+    swap.wait_recv()
+    mine = zown[...] + zr1[...].astype(jnp.float32)
     quarter = half // 4
     zs2[...] = mine.reshape(4, quarter, -1).astype(zs2.dtype)
-    zpart[pl.ds(0, half), :] = mine
+    zown[...] = mine
     sends = []
     for d in range(1, 4):
         to = (z + d) % 4
         sends.append(remote(zs2.at[to], zr2.at[d - 1], sz2.at[d - 1], rz2.at[d - 1], to * 2 + core, c))
         sends[-1].start()
-    total = zpart[pl.ds(z * quarter, quarter), :]
+    total = zown[pl.ds(z * quarter, quarter), :]
     for d in range(1, 4):
         sends[d - 1].wait_recv()
         total = total + zr2[d - 1].astype(jnp.float32)
@@ -333,16 +342,16 @@
         to = (z + d) % 4
         spread.append(remote(own, own, sz3.at[d - 1], rz3.at[d - 1], to * 2 + core, c))
         spread[-1].start()
-    relay = [remote(own, own, sz4.at[0], rz4.at[0], z * 2 + other, c)]
-    relay[0].start()
+    hand = [remote(own, own, sz4.at[0], rz4.at[0], z * 2 + other, c)]
+    hand[0].start()
     for d in range(1, 4):
         spread[d - 1].wait_recv()
         origin = (z + 4 - d) % 4
         part = zfull.at[pl.ds(core * half + origin * quarter, quarter), :]
-        relay.append(remote(part, part, sz4.at[d], rz4.at[d], z * 2 + other, c))
-        relay[-1].start()
+        hand.append(remote(part, part, sz4.at[d], rz4.at[d], z * 2 + other, c))
+        hand[-1].start()
     for d in range(4):
-        relay[d].wait_recv()
+        hand[d].wait_recv()
 
     z1 = zfull[...]
     z2 = jnp.concatenate([-z1[half:], z1[:half]], axis=0)
@@ -433,32 +442,48 @@
         g3[-1].start()
     for d in range(1, 16):
         g3[d - 1].wait_recv()
-    for copy in [pair] + sends + spread + relay + first_a + first_b + second_a + second_b + g1 + g2 + g3:
+    for copy in list(copies.values()) + [pair[s] for s in range(8)]:
         copy.wait_send()
-
-
-def tail(dense_re, dense_im, qt):
+    for s in range(8):
+        for copy in across[s] + back[s] + relay[s]:
+            copy.wait_send()
+    for copy in [swap] + sends + spread + hand + first_a + first_b + second_a + second_b + g1 + g2 + g3:
+        copy.wait_send()
+
+
+def front(reflection, order, q, focus_in, focus_out, ref_angle):
     bf, f32 = jnp.bfloat16, jnp.float32
-    dma = pltpu.SemaphoreType.DMA
-    vm = pltpu.VMEM
+    vm, dma = pltpu.VMEM, pltpu.SemaphoreType.DMA
+    vmem = pl.BlockSpec(memory_space=pltpu.VMEM)
+    anywhere = pl.BlockSpec(memory_space=pl.ANY)
     scratch = [
-        vm((512, 512), f32), vm((256, 512), bf), vm((256, 512), bf), vm((4, 64, 512), bf), vm((3, 64, 512), bf), vm((512, 512), bf),
+        vm((4, 4, 2, 64, 2048), bf), vm((2, 2048, 512), bf), vm((2, 1024, 1024), bf), vm((1024, 512), f32), vm((1024, 512), f32),
+        vm((8, 2, 4, 32, 512), f32), vm((8, 4, 32, 512), f32), vm((8, 4, 32, 512), f32), vm((8, 3, 32, 512), f32), vm((2, 1024, 512), bf),
+        vm((4, 32, 512), bf), vm((4, 32, 512), bf), vm((4, 32, 512), bf), vm((3, 32, 512), bf),
+        vm((2, 1024, 512), f32), vm((1024, 512), bf), vm((1024, 512), bf),
+        vm((2, RANK, 1024), bf), vm((256, 512), f32), vm((256, 512), bf), vm((256, 512), bf), vm((4, 64, 512), bf), vm((3, 64, 512), bf), vm((512, 512), bf),
         vm((4, 64, 256), f32), vm((4, 4, 64, 256), f32), vm((3, 4, 64, 256), bf), vm((4, 4, 64, 256), bf),
-        vm((3, 4, 64, 256), bf), vm((3, 4, 64, 256), bf), vm((2, 4, 64, 256), f32), vm((3, 64, 256), f32), vm((3, 64, 256), f32),
+        vm((3, 4, 64, 256), bf), vm((3, 4, 64, 256), bf), vm((2, 4, 64, 256), bf), vm((3, 64, 256), bf), vm((3, 64, 256), bf),
         vm((16, 16, RANK), f32), vm((15, 16, RANK), f32), vm((8, 16, RANK), f32),
+        dma((3,)), dma((40,)), dma((40,)), dma((8,)), dma((8,)), dma((8, 3)), dma((8, 3)), dma((8, 3)), dma((8, 3)), dma((8, 4)), dma((8, 4)),
         dma, dma, dma((3,)), dma((3,)), dma((3,)), dma((3,)), dma((4,)), dma((4,)), dma((3,)), dma((3,)), dma((3,)), dma((3,)),
         dma((3,)), dma((3,)), dma((3,)), dma((3,)), dma((15,)), dma((15,)), dma((7,)), dma((7,)), dma((15,)), dma((15,)),
     ]
-    vmem = pl.BlockSpec(memory_space=pltpu.VMEM)
     return pl.pallas_call(
-        tail_kernel,
+        front_kernel,
         out_shape=(jax.ShapeDtypeStruct((64, 2 * RANK), f32), jax.ShapeDtypeStruct((16, 16, RANK), f32)),
-        in_specs=[vmem] * 3,
+        in_specs=[vmem, vmem, vmem, anywhere, anywhere, anywhere],
         out_specs=(vmem, vmem),
         scratch_shapes=scratch,
-        compiler_params=pltpu.CompilerParams(collective_id=1, has_side_effects=True, vmem_limit_bytes=48 << 20),
-    )(dense_re, dense_im, qt)
-
+        compiler_params=pltpu.CompilerParams(collective_id=0, has_side_effects=True, vmem_limit_bytes=62 << 20),
+    )(reflection, order, q, focus_in, focus_out, ref_angle)
+
+
+def bc(w, j):
+    return jnp.broadcast_to(w[:, j:j+1], w.shape)
+
+def rowb(w, j):
+    return jnp.broadcast_to(w[j:j+1, :], w.shape)
 
 def factor_inverse(diag):
     lane = lax.broadcasted_iota(jnp.int32, (NB, 4 * NB), 1)
@@ -469,17 +494,42 @@
     z = jnp.zeros((NB, 2 * NB), jnp.float32)
     w = jnp.concatenate([re, im, z], axis=1) + unit
     v = jnp.concatenate([-im, re, z], axis=1) + unit_i
-    sub1 = sub[:, :1]
-    for j in range(NB - 1):
-        piv = w[j : j + 1, j : j + 1]
-        below = sub1 > j
-        c_re = jnp.where(below, w[:, j : j + 1], 0.0)
-        c_im = jnp.where(below, w[:, NB + j : NB + j + 1], 0.0)
-        inv = 1.0 / piv
-        row = w[j : j + 1, :] * inv
-        rov = v[j : j + 1, :] * inv
-        w = w - (c_re * row + c_im * rov)
-        v = v - (c_re * rov - c_im * row)
+    for base in range(0, NB, 8):
+        cols = [(bc(w, j), bc(w, NB + j)) for j in range(base, base + 8)]
+        while cols:
+            (a_re, a_im), (b_re, b_im) = cols[:2]
+            cols = cols[2:]
+            j = base + 8 - len(cols) - 2
+            p, q = a_re[j : j + 1], b_re[j + 1 : j + 2]
+            s_re, s_im = a_re[j + 1 : j + 2], a_im[j + 1 : j + 2]
+            det = 1.0 / (p * q - (s_re * s_re + s_im * s_im))
+            pd, qd, sd_re, sd_im = p * det, q * det, s_re * det, s_im * det
+            after = []
+            for c_re, c_im in cols:
+                x_re, x_im, y_re, y_im = c_re[j : j + 1], c_im[j : j + 1], c_re[j + 1 : j + 2], c_im[j + 1 : j + 2]
+                g_re = qd * x_re - (sd_re * y_re + sd_im * y_im)
+                g_im = qd * x_im - (sd_re * y_im - sd_im * y_re)
+                h_re = pd * y_re - (sd_re * x_re - sd_im * x_im)
+                h_im = pd * y_im - (sd_re * x_im + sd_im * x_re)
+                after.append((
+                    c_re - ((a_re * g_re - a_im * g_im) + (b_re * h_re - b_im * h_im)),
+                    c_im - ((a_re * g_im + a_im * g_re) + (b_re * h_im + b_im * h_re)),
+                ))
+            cols = after
+            top = 1.0 / p
+            w0, v0, w1, v1 = w[j : j + 1, :], v[j : j + 1, :], w[j + 1 : j + 2, :], v[j + 1 : j + 2, :]
+            u0 = qd * w0 - (sd_re * w1 - sd_im * v1)
+            t0 = qd * v0 - (sd_re * v1 + sd_im * w1)
+            u1 = pd * w1 - (sd_re * w0 + sd_im * v0)
+            t1 = pd * v1 - (sd_re * v0 - sd_im * w0)
+            second = sub == j + 1
+            below = sub > j + 1
+            x0, y0 = (s_re * w0 + s_im * v0) * top, (s_re * v0 - s_im * w0) * top
+            dw = (a_re * u0 + a_im * t0) + (b_re * u1 + b_im * t1)
+            dv = (a_re * t0 - a_im * u0) + (b_re * t1 - b_im * u1)
+            w = w - jnp.where(below, dw, jnp.where(second, x0, 0.0))
+            v = v - jnp.where(below, dv, jnp.where(second, y0, 0.0))
+
     d = jnp.sum(jnp.where(lane == sub, w, 0.0), axis=1, keepdims=True)
     return w[:, 2 * NB :] * lax.rsqrt(d)
 
@@ -503,16 +553,20 @@
         a_ref[:n, 2 * NB * k + NB : 2 * NB * (k + 1)] = g_im[:, NB * k : NB * k + NB]
         a_ref[n:, 2 * NB * k : 2 * NB * k + NB] = y_ref[:, NB * k : NB * k + NB]
         a_ref[n:, 2 * NB * k + NB : 2 * NB * (k + 1)] = y_ref[:, n + NB * k : n + NB * k + NB]
+    diag = a_ref[:NB, : 2 * NB]
     for k in range(panels):
         lo = k * NB
-        inv = factor_inverse(a_ref[lo : lo + NB, 2 * lo : 2 * lo + 2 * NB])
+        inv = factor_inverse(diag)
         both = jnp.concatenate([inv, swapped(inv)], axis=0)
-        ap = a_ref[lo + NB :, 2 * lo : 2 * lo + 2 * NB]
-        low = dot_nt(ap, both, HI)
+        left = panels - 1 - k
+        if left:
+            nxt = dot_nt(a_ref[lo + NB : lo + 2 * NB, 2 * lo : 2 * lo + 2 * NB], both, HI)
+            turn = jnp.concatenate([nxt, swapped(nxt)], axis=0)
+            diag = a_ref[lo + NB : lo + 2 * NB, 2 * lo + 2 * NB : 2 * lo + 4 * NB] - dot_nt(nxt, turn, HI)
+        low = dot_nt(a_ref[lo + NB :, 2 * lo : 2 * lo + 2 * NB], both, HI)
         solved = low[low.shape[0] - rows :] * scale
         out_ref[:, 0, lo : lo + NB] = solved[:, :NB]
         out_ref[:, 1, lo : lo + NB] = solved[:, NB:]
-        left = panels - 1 - k
         if left:
             lk = low[: left * NB]
             q = jnp.concatenate([lk.reshape(left, NB, 2 * NB), swapped(lk).reshape(left, NB, 2 * NB)], axis=1)
@@ -532,9 +586,7 @@
 
 
 def body(reflection, focus_in, focus_out, ref_angle, element_order, q_start):
-    dense_re, dense_im = head(reflection, element_order.reshape(1, -1), focus_in, focus_out, ref_angle)
-    qt = jnp.transpose(q_start, (1, 2, 0)).reshape(2 * RANK, -1)
-    image, gram = tail(dense_re, dense_im, qt)
+    image, gram = front(reflection, element_order.reshape(1, -1), q_start, focus_in, focus_out, ref_angle)
     return chol(gram.reshape(RANK, RANK), image, math.sqrt(NF))
 
 

time: 165 us -> 138 us (0.84)
  Pallas kernels: 159 us -> 138 us
  local copies, waits for them, and re-layouts: 6.22 us -> 0 us
    pallas_call x1, Pallas kernels: 31.2 us -> 16.8 us  [chol(): pl.pallas_call(functools.partial(chol_kernel, scale), out_shape=jax.Shape...]
    pallas_call x2 -> x1, Pallas kernels: 128 us -> 121 us  [front(): pl.pallas_call(front_kernel, out_shape=(jax.ShapeDtypeStruct((64, 2 * RAN...]
    unnamed x8 -> x0, local copies, waits for them, and re-layouts: 3.78 us -> none
    transpose x1 -> x0, local copies, waits for them, and re-layouts: 2.45 us -> none  [body(): qt = jnp.transpose(q_start, (1, 2, 0)).reshape(2 * RANK, -1)]
where the time goes in v4:
time: 138 us
  Pallas kernels  138 us (100%)
    pallas_call x1, Pallas kernels, front(): pl.pallas_call(front_kernel, out_shape=(jax.ShapeDtypeStruct((64, 2 * RAN...  121 us
    pallas_call x1, Pallas kernels, chol(): pl.pallas_call(functools.partial(chol_kernel, scale), out_shape=jax.Shape...  16.8 us

profile of v4, /device:TPU:0, one launch (start us, length us, event | category | flops | bytes accessed | tf_op | source)
XLA Modules:
  0.0 138.1 jit_solution(16678814510434594227)
XLA Ops:
  0.0 121.3 %shard_map.64 = (f32[64,512]{1,0:T(8,128)}, f32[16,16,256]{2,1,0:T(8,128)}) custom-call(bf16[2,64,2048]{2,1,0:T(8,128)(2,1)} %refl_ref.1, s32[1,2048]{1,0:T(1,128)} %bitcast.3, bf16[1024,2,256]{2,1,0:T(2,128)(2,1)} %q_ref.1, bf16[2,2048,512]{2,1,0:T(8,128)(2,1)} %focus_in_hbm.1, bf16[2,1024,1024]{2,1,0:T(8,128)(2,1)} %focus_out_hbm.1, f32[1024,512]{1,0:T(8,128)} %angle_hbm.1), custom_call_target="tpu_custom_call" | custom-call | tf_op jit(solution)/shard_map/pallas_call | solution.py:472
  121.3 16.8 %shard_map.65 = f32[64,2,256]{2,1,0:T(2,128)} custom-call(f32[256,256]{1,0:T(8,128)} %bitcast.2, f32[64,512]{1,0:T(8,128)} %get-tuple-element.8.y_ref), custom_call_target="tpu_custom_call" | custom-call | tf_op jit(solution)/shard_map/pallas_call | solution.py:579

commit v5 on v4

--- a/solution.py
+++ b/solution.py
@@ -11,7 +11,7 @@
 NF = 8192
 RANK = 256
 PANEL_W = 512
-NB = 32
+NB = 64
 HI = lax.Precision.HIGHEST
 MESH = pl.DeviceIdType.MESH
 
@@ -187,8 +187,8 @@
         [(left, low, 0), (left, high, 0), (left, low, 1), (right, low, 1)],
         [(right, low, 0), (right, high, 0), (left, high, 1), (right, high, 1)],
         [(x, far_y, 0), (far_x, y, 1), (far_x, low, 0), (far_x, high, 0)],
-        [(left, far_y, 1), (right, far_y, 1), (left, far_y, 0), (far_x, low, 1)],
-        [(right, far_y, 0), (far_x, high, 1), (far_x, far_y, 0), (far_x, far_y, 1)],
+        [(left, far_y, 1), (right, far_y, 1), (left, far_y, 0), (right, far_y, 0)],
+        [(far_x, low, 1), (far_x, high, 1), (far_x, far_y, 0), (far_x, far_y, 1)],
     ]
 
     def progress(s):
@@ -252,9 +252,9 @@
             send("Bq3x+", left, far_y, 1, 0)
             send("Bq3x-", right, far_y, 1, 1)
         elif s == 6:
-            got("Aq1y", "Bq1x")
+            got("Aq1y", "Aq2y")
         else:
-            got("Aq2y", "Bq2x", "Aq3y", "Bq3x")
+            got("Bq1x", "Bq2x", "Aq3y", "Bq3x")
         progress(s)
         gemm(s, batches[s])
         start_pair(s)
@@ -291,9 +291,10 @@
     @pl.loop(0, 8)
     def _(m):
         rows = pl.ds(pl.multiple_of(m * 128, 128), 128)
-        add_re, add_im = outer(left, rows)
-        acc[0, rows, :] += add_re
-        acc[1, rows, :] += add_im
+        left_re, left_im = outer(left, rows)
+        right_re, right_im = outer(right, rows)
+        acc[0, rows, :] += left_re + right_re
+        acc[1, rows, :] += left_im + right_im
 
     start_relay(7, batches[7])
     finish(7)
@@ -301,10 +302,9 @@
     @pl.loop(0, 8)
     def _(m):
         rows = pl.ds(pl.multiple_of(m * 128, 128), 128)
-        right_re, right_im = outer(right, rows)
         far_re, far_im = outer(far_x, rows)
-        outer_re = acc[0, rows, :] + (right_re + far_re)
-        outer_im = acc[1, rows, :] + (right_im + far_im)
+        outer_re = acc[0, rows, :] + far_re
+        outer_im = acc[1, rows, :] + far_im
         co, si = cosine[rows, :], sine[rows, :]
         dense_re[rows, :] = (outer_re * co + outer_im * si).astype(jnp.bfloat16)
         dense_im[rows, :] = (outer_im * co - outer_re * si).astype(jnp.bfloat16)
@@ -353,32 +353,31 @@
     for d in range(4):
         hand[d].wait_recv()
 
-    z1 = zfull[...]
-    z2 = jnp.concatenate([-z1[half:], z1[:half]], axis=0)
-    first_a = []
-    for d in (1, 2, 3, 0):
+    z_re, z_im = zfull.at[pl.ds(0, half), :], zfull.at[pl.ds(half, half), :]
+    first_a, first_b = {}, {}
+    for d in (2, 1, 3, 0):
         to = (x + d) % 4
         rows = pl.ds(to * 256, 256)
-        block = dot_nt(dense_re[rows, :], z1) + dot_nt(dense_im[rows, :], z2)
-        block_a = block[:, :half].reshape(4, 64, half)
-        block_b = block[:, half:].reshape(4, 64, half)
-        for j in range(4):
-            ysb[j, to] = block_b[j].astype(ysb.dtype)
-            yown_b[j, to] = block_b[j]
+        block = (dot_nt(dense_re[rows, :], z_re[...]) - dot_nt(dense_im[rows, :], z_im[...])).reshape(4, 64, half)
         if d:
-            ysa[d - 1] = block_a.astype(ysa.dtype)
-            first_a.append(remote(ysa.at[d - 1], yra.at[d - 1], sya.at[d - 1], rya.at[d - 1], r, to * 4 + y))
-            first_a[-1].start()
+            ysa[d - 1] = block.astype(ysa.dtype)
+            first_a[d] = remote(ysa.at[d - 1], yra.at[d - 1], sya.at[d - 1], rya.at[d - 1], r, to * 4 + y)
+            first_a[d].start()
         else:
-            yown_a[...] = block_a
-    first_b = []
-    for d in range(1, 4):
+            yown_a[...] = block
         to = (y + d) % 4
-        first_b.append(remote(ysb.at[to], yrb.at[d - 1], syb.at[d - 1], ryb.at[d - 1], r, x * 4 + to))
-        first_b[-1].start()
+        rows_re = jnp.concatenate([dense_re[pl.ds(i * 256 + to * 64, 64), :] for i in range(4)], axis=0)
+        rows_im = jnp.concatenate([dense_im[pl.ds(i * 256 + to * 64, 64), :] for i in range(4)], axis=0)
+        block = (dot_nt(rows_re, z_im[...]) + dot_nt(rows_im, z_re[...])).reshape(4, 64, half)
+        if d:
+            ysb[d - 1] = block.astype(ysb.dtype)
+            first_b[d] = remote(ysb.at[d - 1], yrb.at[d - 1], syb.at[d - 1], ryb.at[d - 1], r, x * 4 + to)
+            first_b[d].start()
+        else:
+            yown_b[...] = block
     sum_a = yown_a[...]
     for d in range(1, 4):
-        first_a[d - 1].wait_recv()
+        first_a[d].wait_recv()
         sum_a = sum_a + yra[d - 1].astype(jnp.float32)
     yown_a[...] = sum_a
     ys2[0] = sum_a.astype(ys2.dtype)
@@ -387,11 +386,11 @@
         to = (y + d) % 4
         second_a.append(remote(ys2.at[0, to], yr2a.at[d - 1], sy2a.at[d - 1], ry2a.at[d - 1], r, x * 4 + to))
         second_a[-1].start()
-    sum_b = yown_b[y]
-    for d in range(1, 4):
-        first_b[d - 1].wait_recv()
+    sum_b = yown_b[...]
+    for d in range(1, 4):
+        first_b[d].wait_recv()
         sum_b = sum_b + yrb[d - 1].astype(jnp.float32)
-    yown_b[0] = sum_b
+    yown_b[...] = sum_b
     ys2[1] = sum_b.astype(ys2.dtype)
     second_b = []
     for d in range(1, 4):
@@ -402,7 +401,7 @@
     for d in range(1, 4):
         second_a[d - 1].wait_recv()
         final_a = final_a + yr2a[d - 1].astype(jnp.float32)
-    final_b = yown_b[0, x]
+    final_b = yown_b[x]
     for d in range(1, 4):
         second_b[d - 1].wait_recv()
         final_b = final_b + yr2b[d - 1].astype(jnp.float32)
@@ -416,9 +415,11 @@
     rows = lax.broadcasted_iota(jnp.int32, (RANK, RANK), 0)
     cols = lax.broadcasted_iota(jnp.int32, (RANK, RANK), 1)
     hpart[...] = jnp.where(rows >= cols, gram_re, gram_im).reshape(16, 16, RANK)
+    steps = sorted(((i, j) for i in range(4) for j in range(4) if i or j), key=lambda p: -min(p[0], 4 - p[0]) - min(p[1], 4 - p[1]))
+    columns = [(x + i) % 4 * 4 + (y + j) % 4 for i, j in steps]
     g1 = []
     for d in range(1, 16):
-        to = (c + d) % 16
+        to = columns[d - 1]
         g1.append(remote(hpart.at[to], hrecv.at[d - 1], sh1.at[d - 1], rh1.at[d - 1], r, to))
         g1[-1].start()
     acc = hpart[c]
@@ -438,7 +439,7 @@
     gram_ref[c] = acc
     g3 = []
     for d in range(1, 16):
-        g3.append(remote(gram_ref.at[c], gram_ref.at[c], sh3.at[d - 1], rh3.at[d - 1], r, (c + d) % 16))
+        g3.append(remote(gram_ref.at[c], gram_ref.at[c], sh3.at[d - 1], rh3.at[d - 1], r, columns[d - 1]))
         g3[-1].start()
     for d in range(1, 16):
         g3[d - 1].wait_recv()
@@ -447,7 +448,7 @@
     for s in range(8):
         for copy in across[s] + back[s] + relay[s]:
             copy.wait_send()
-    for copy in [swap] + sends + spread + hand + first_a + first_b + second_a + second_b + g1 + g2 + g3:
+    for copy in [swap] + sends + spread + hand + list(first_a.values()) + list(first_b.values()) + second_a + second_b + g1 + g2 + g3:
         copy.wait_send()
 
 
@@ -462,7 +463,7 @@
         vm((4, 32, 512), bf), vm((4, 32, 512), bf), vm((4, 32, 512), bf), vm((3, 32, 512), bf),
         vm((2, 1024, 512), f32), vm((1024, 512), bf), vm((1024, 512), bf),
         vm((2, RANK, 1024), bf), vm((256, 512), f32), vm((256, 512), bf), vm((256, 512), bf), vm((4, 64, 512), bf), vm((3, 64, 512), bf), vm((512, 512), bf),
-        vm((4, 64, 256), f32), vm((4, 4, 64, 256), f32), vm((3, 4, 64, 256), bf), vm((4, 4, 64, 256), bf),
+        vm((4, 64, 256), f32), vm((4, 64, 256), f32), vm((3, 4, 64, 256), bf), vm((3, 4, 64, 256), bf),
         vm((3, 4, 64, 256), bf), vm((3, 4, 64, 256), bf), vm((2, 4, 64, 256), bf), vm((3, 64, 256), bf), vm((3, 64, 256), bf),
         vm((16, 16, RANK), f32), vm((15, 16, RANK), f32), vm((8, 16, RANK), f32),
         dma((3,)), dma((40,)), dma((40,)), dma((8,)), dma((8,)), dma((8, 3)), dma((8, 3)), dma((8, 3)), dma((8, 3)), dma((8, 4)), dma((8, 4)),
@@ -479,59 +480,61 @@
     )(reflection, order, q, focus_in, focus_out, ref_angle)
 
 
-def bc(w, j):
-    return jnp.broadcast_to(w[:, j:j+1], w.shape)
-
-def rowb(w, j):
-    return jnp.broadcast_to(w[j:j+1, :], w.shape)
+def column(m, j):
+    return jnp.broadcast_to(m[:, j : j + 1], m.shape)
+
+
+def times_i_rows(m):
+    return jnp.concatenate([-m[:, NB : 2 * NB], m[:, :NB], -m[:, 3 * NB :], m[:, 2 * NB : 3 * NB]], axis=1)
+
 
 def factor_inverse(diag):
     lane = lax.broadcasted_iota(jnp.int32, (NB, 4 * NB), 1)
     sub = lax.broadcasted_iota(jnp.int32, (NB, 4 * NB), 0)
-    unit = (lane - 2 * NB == sub).astype(jnp.float32)
-    unit_i = (lane - 3 * NB == sub).astype(jnp.float32)
-    re, im = diag[:, :NB], diag[:, NB:]
-    z = jnp.zeros((NB, 2 * NB), jnp.float32)
-    w = jnp.concatenate([re, im, z], axis=1) + unit
-    v = jnp.concatenate([-im, re, z], axis=1) + unit_i
+    w = jnp.concatenate([diag, jnp.zeros_like(diag)], axis=1) + (lane - 2 * NB == sub).astype(jnp.float32)
+    row = lax.broadcasted_iota(jnp.int32, (8, 4 * NB), 0)
+    done = []
     for base in range(0, NB, 8):
-        cols = [(bc(w, j), bc(w, NB + j)) for j in range(base, base + 8)]
-        while cols:
-            (a_re, a_im), (b_re, b_im) = cols[:2]
-            cols = cols[2:]
-            j = base + 8 - len(cols) - 2
+        top, under = w[:8], w[8:]
+        more = under.shape[0] > 0
+        turn = times_i_rows(top)
+        cols = [(column(w, base + j), column(w, NB + base + j)) for j in range(8)]
+        for j in range(0, 8, 2):
+            (a_re, a_im), (b_re, b_im) = cols[j : j + 2]
             p, q = a_re[j : j + 1], b_re[j + 1 : j + 2]
             s_re, s_im = a_re[j + 1 : j + 2], a_im[j + 1 : j + 2]
             det = 1.0 / (p * q - (s_re * s_re + s_im * s_im))
             pd, qd, sd_re, sd_im = p * det, q * det, s_re * det, s_im * det
-            after = []
-            for c_re, c_im in cols:
+            for m in range(j + 2, 8):
+                c_re, c_im = cols[m]
                 x_re, x_im, y_re, y_im = c_re[j : j + 1], c_im[j : j + 1], c_re[j + 1 : j + 2], c_im[j + 1 : j + 2]
                 g_re = qd * x_re - (sd_re * y_re + sd_im * y_im)
                 g_im = qd * x_im - (sd_re * y_im - sd_im * y_re)
                 h_re = pd * y_re - (sd_re * x_re - sd_im * x_im)
                 h_im = pd * y_im - (sd_re * x_im + sd_im * x_re)
-                after.append((
+                cols[m] = (
                     c_re - ((a_re * g_re - a_im * g_im) + (b_re * h_re - b_im * h_im)),
                     c_im - ((a_re * g_im + a_im * g_re) + (b_re * h_im + b_im * h_re)),
-                ))
-            cols = after
-            top = 1.0 / p
-            w0, v0, w1, v1 = w[j : j + 1, :], v[j : j + 1, :], w[j + 1 : j + 2, :], v[j + 1 : j + 2, :]
+                )
+            w0, v0, w1, v1 = top[j : j + 1], turn[j : j + 1], top[j + 1 : j + 2], turn[j + 1 : j + 2]
             u0 = qd * w0 - (sd_re * w1 - sd_im * v1)
             t0 = qd * v0 - (sd_re * v1 + sd_im * w1)
             u1 = pd * w1 - (sd_re * w0 + sd_im * v0)
             t1 = pd * v1 - (sd_re * v0 - sd_im * w0)
-            second = sub == j + 1
-            below = sub > j + 1
-            x0, y0 = (s_re * w0 + s_im * v0) * top, (s_re * v0 - s_im * w0) * top
-            dw = (a_re * u0 + a_im * t0) + (b_re * u1 + b_im * t1)
-            dv = (a_re * t0 - a_im * u0) + (b_re * t1 - b_im * u1)
-            w = w - jnp.where(below, dw, jnp.where(second, x0, 0.0))
-            v = v - jnp.where(below, dv, jnp.where(second, y0, 0.0))
-
-    d = jnp.sum(jnp.where(lane == sub, w, 0.0), axis=1, keepdims=True)
-    return w[:, 2 * NB :] * lax.rsqrt(d)
+            inv = 1.0 / p
+            x0, y0 = (s_re * w0 + s_im * v0) * inv, (s_re * v0 - s_im * w0) * inv
+            if more:
+                d_re, d_im, e_re, e_im = a_re[8:], a_im[8:], b_re[8:], b_im[8:]
+                under = under - ((d_re * u0 + d_im * t0) + (e_re * u1 + e_im * t1))
+            d_re, d_im, e_re, e_im = a_re[:8], a_im[:8], b_re[:8], b_im[:8]
+            dw = (d_re * u0 + d_im * t0) + (e_re * u1 + e_im * t1)
+            dv = (d_re * t0 - d_im * u0) + (e_re * t1 - e_im * u1)
+            top = top - jnp.where(row > j + 1, dw, jnp.where(row == j + 1, x0, 0.0))
+            turn = turn - jnp.where(row > j + 1, dv, jnp.where(row == j + 1, y0, 0.0))
+        d = jnp.sum(jnp.where(lane[:8] == row + base, top, 0.0), axis=1, keepdims=True)
+        done.append(top[:, 2 * NB :] * lax.rsqrt(d))
+        w = under
+    return jnp.concatenate(done, axis=0)
 
 
 def swapped(m):

time: 138 us -> 136 us (0.986)
  Pallas kernels: 138 us -> 136 us
    pallas_call x1, Pallas kernels: 16.8 us -> 14.9 us  [chol(): pl.pallas_call(functools.partial(chol_kernel, scale), out_shape=jax.Shape...]
where the time goes in v5:
time: 136 us
  Pallas kernels  136 us (100%)
    pallas_call x1, Pallas kernels, front(): pl.pallas_call(front_kernel, out_shape=(jax.ShapeDtypeStruct((64, 2 * RAN...  121 us
    pallas_call x1, Pallas kernels, chol(): pl.pallas_call(functools.partial(chol_kernel, scale), out_shape=jax.Shape...  14.9 us

profile of v5, /device:TPU:0, one launch (start us, length us, event | category | flops | bytes accessed | tf_op | source)
XLA Modules:
  0.0 135.6 jit_solution(14570160725201940094)
XLA Ops:
  0.0 120.7 %shard_map.64 = (f32[64,512]{1,0:T(8,128)}, f32[16,16,256]{2,1,0:T(8,128)}) custom-call(bf16[2,64,2048]{2,1,0:T(8,128)(2,1)} %refl_ref.1, s32[1,2048]{1,0:T(1,128)} %bitcast.3, bf16[1024,2,256]{2,1,0:T(2,128)(2,1)} %q_ref.1, bf16[2,2048,512]{2,1,0:T(8,128)(2,1)} %focus_in_hbm.1, bf16[2,1024,1024]{2,1,0:T(8,128)(2,1)} %focus_out_hbm.1, f32[1024,512]{1,0:T(8,128)} %angle_hbm.1), custom_call_target="tpu_custom_call" | custom-call | tf_op jit(solution)/shard_map/pallas_call | solution.py:473
  120.7 14.9 %shard_map.65 = f32[64,2,256]{2,1,0:T(2,128)} custom-call(f32[256,256]{1,0:T(8,128)} %bitcast.2, f32[64,512]{1,0:T(8,128)} %get-tuple-element.8.y_ref), custom_call_target="tpu_custom_call" | custom-call | tf_op jit(solution)/shard_map/pallas_call | solution.py:582

commit v6 on v5

--- a/solution.py
+++ b/solution.py
@@ -317,41 +317,44 @@
 
     sign = (1 - 2 * core).astype(jnp.float32)
     zs1[...] = z_half(other, -sign).astype(jnp.bfloat16)
-    swap = remote(zs1, zr1, sz1, rz1, z * 2 + other, c)
-    swap.start()
+    eighth = half // 8
+    swap, sends, spread, hand = [], [], [], []
+    for g in range(2):
+        part = pl.ds(g * 4 * eighth, 4 * eighth)
+        swap.append(remote(zs1.at[part, :], zr1.at[part, :], sz1.at[g], rz1.at[g], z * 2 + other, c))
+        swap[g].start()
     zown[...] = z_half(core, sign)
-    swap.wait_recv()
-    mine = zown[...] + zr1[...].astype(jnp.float32)
-    quarter = half // 4
-    zs2[...] = mine.reshape(4, quarter, -1).astype(zs2.dtype)
-    zown[...] = mine
-    sends = []
-    for d in range(1, 4):
-        to = (z + d) % 4
-        sends.append(remote(zs2.at[to], zr2.at[d - 1], sz2.at[d - 1], rz2.at[d - 1], to * 2 + core, c))
-        sends[-1].start()
-    total = zown[pl.ds(z * quarter, quarter), :]
-    for d in range(1, 4):
-        sends[d - 1].wait_recv()
-        total = total + zr2[d - 1].astype(jnp.float32)
-    slot = core * half + z * quarter
-    own = zfull.at[pl.ds(slot, quarter), :]
-    zfull[pl.ds(slot, quarter), :] = total.astype(jnp.bfloat16)
-    spread = []
-    for d in range(1, 4):
-        to = (z + d) % 4
-        spread.append(remote(own, own, sz3.at[d - 1], rz3.at[d - 1], to * 2 + core, c))
-        spread[-1].start()
-    hand = [remote(own, own, sz4.at[0], rz4.at[0], z * 2 + other, c)]
-    hand[0].start()
-    for d in range(1, 4):
-        spread[d - 1].wait_recv()
-        origin = (z + 4 - d) % 4
-        part = zfull.at[pl.ds(core * half + origin * quarter, quarter), :]
-        hand.append(remote(part, part, sz4.at[d], rz4.at[d], z * 2 + other, c))
+    for g in range(2):
+        part = pl.ds(g * 4 * eighth, 4 * eighth)
+        swap[g].wait_recv()
+        mine = zown[part, :] + zr1[part, :].astype(jnp.float32)
+        zs2[g] = mine.reshape(4, eighth, -1).astype(zs2.dtype)
+        zown[part, :] = mine
+        for d in range(1, 4):
+            to = (z + d) % 4
+            sends.append(remote(zs2.at[g, to], zr2.at[g, d - 1], sz2.at[g, d - 1], rz2.at[g, d - 1], to * 2 + core, c))
+            sends[-1].start()
+    for g in range(2):
+        total = zown[pl.ds((g * 4 + z) * eighth, eighth), :]
+        for d in range(1, 4):
+            sends[3 * g + d - 1].wait_recv()
+            total = total + zr2[g, d - 1].astype(jnp.float32)
+        slot = core * half + (g * 4 + z) * eighth
+        zfull[pl.ds(slot, eighth), :] = total.astype(jnp.bfloat16)
+        own = zfull.at[pl.ds(slot, eighth), :]
+        for d in range(1, 4):
+            spread.append(remote(own, own, sz3.at[g, d - 1], rz3.at[g, d - 1], (z + d) % 4 * 2 + core, c))
+            spread[-1].start()
+        hand.append(remote(own, own, sz4.at[g, 0], rz4.at[g, 0], z * 2 + other, c))
         hand[-1].start()
-    for d in range(4):
-        hand[d].wait_recv()
+    for g in range(2):
+        for d in range(1, 4):
+            spread[3 * g + d - 1].wait_recv()
+            part = zfull.at[pl.ds(core * half + (g * 4 + (z + 4 - d) % 4) * eighth, eighth), :]
+            hand.append(remote(part, part, sz4.at[g, d], rz4.at[g, d], z * 2 + other, c))
+            hand[-1].start()
+    for copy in hand:
+        copy.wait_recv()
 
     z_re, z_im = zfull.at[pl.ds(0, half), :], zfull.at[pl.ds(half, half), :]
     first_a, first_b = {}, {}
@@ -448,7 +451,7 @@
     for s in range(8):
         for copy in across[s] + back[s] + relay[s]:
             copy.wait_send()
-    for copy in [swap] + sends + spread + hand + list(first_a.values()) + list(first_b.values()) + second_a + second_b + g1 + g2 + g3:
+    for copy in swap + sends + spread + hand + list(first_a.values()) + list(first_b.values()) + second_a + second_b + g1 + g2 + g3:
         copy.wait_send()
 
 
@@ -462,12 +465,12 @@
         vm((8, 2, 4, 32, 512), f32), vm((8, 4, 32, 512), f32), vm((8, 4, 32, 512), f32), vm((8, 3, 32, 512), f32), vm((2, 1024, 512), bf),
         vm((4, 32, 512), bf), vm((4, 32, 512), bf), vm((4, 32, 512), bf), vm((3, 32, 512), bf),
         vm((2, 1024, 512), f32), vm((1024, 512), bf), vm((1024, 512), bf),
-        vm((2, RANK, 1024), bf), vm((256, 512), f32), vm((256, 512), bf), vm((256, 512), bf), vm((4, 64, 512), bf), vm((3, 64, 512), bf), vm((512, 512), bf),
+        vm((2, RANK, 1024), bf), vm((256, 512), f32), vm((256, 512), bf), vm((256, 512), bf), vm((2, 4, 32, 512), bf), vm((2, 3, 32, 512), bf), vm((512, 512), bf),
         vm((4, 64, 256), f32), vm((4, 64, 256), f32), vm((3, 4, 64, 256), bf), vm((3, 4, 64, 256), bf),
         vm((3, 4, 64, 256), bf), vm((3, 4, 64, 256), bf), vm((2, 4, 64, 256), bf), vm((3, 64, 256), bf), vm((3, 64, 256), bf),
         vm((16, 16, RANK), f32), vm((15, 16, RANK), f32), vm((8, 16, RANK), f32),
         dma((3,)), dma((40,)), dma((40,)), dma((8,)), dma((8,)), dma((8, 3)), dma((8, 3)), dma((8, 3)), dma((8, 3)), dma((8, 4)), dma((8, 4)),
-        dma, dma, dma((3,)), dma((3,)), dma((3,)), dma((3,)), dma((4,)), dma((4,)), dma((3,)), dma((3,)), dma((3,)), dma((3,)),
+        dma((2,)), dma((2,)), dma((2, 3)), dma((2, 3)), dma((2, 3)), dma((2, 3)), dma((2, 4)), dma((2, 4)), dma((3,)), dma((3,)), dma((3,)), dma((3,)),
         dma((3,)), dma((3,)), dma((3,)), dma((3,)), dma((15,)), dma((15,)), dma((7,)), dma((7,)), dma((15,)), dma((15,)),
     ]
     return pl.pallas_call(

time: 136 us -> 134 us (0.985)
  Pallas kernels: 136 us -> 134 us
    pallas_call x1, Pallas kernels: 121 us -> 119 us  [front(): pl.pallas_call(front_kernel, out_shape=(jax.ShapeDtypeStruct((64, 2 * RAN...]
where the time goes in v6:
time: 134 us
  Pallas kernels  134 us (100%)
    pallas_call x1, Pallas kernels, front(): pl.pallas_call(front_kernel, out_shape=(jax.ShapeDtypeStruct((64, 2 * RAN...  119 us
    pallas_call x1, Pallas kernels, chol(): pl.pallas_call(functools.partial(chol_kernel, scale), out_shape=jax.Shape...  14.9 us

profile of v6, /device:TPU:0, one launch (start us, length us, event | category | flops | bytes accessed | tf_op | source)
XLA Modules:
  0.0 133.9 jit_solution(11464331136160239367)
XLA Ops:
  0.0 119.0 %shard_map.64 = (f32[64,512]{1,0:T(8,128)}, f32[16,16,256]{2,1,0:T(8,128)}) custom-call(bf16[2,64,2048]{2,1,0:T(8,128)(2,1)} %refl_ref.1, s32[1,2048]{1,0:T(1,128)} %bitcast.3, bf16[1024,2,256]{2,1,0:T(2,128)(2,1)} %q_ref.1, bf16[2,2048,512]{2,1,0:T(8,128)(2,1)} %focus_in_hbm.1, bf16[2,1024,1024]{2,1,0:T(8,128)(2,1)} %focus_out_hbm.1, f32[1024,512]{1,0:T(8,128)} %angle_hbm.1), custom_call_target="tpu_custom_call" | custom-call | tf_op jit(solution)/shard_map/pallas_call | solution.py:476
  119.0 14.9 %shard_map.65 = f32[64,2,256]{2,1,0:T(2,128)} custom-call(f32[256,256]{1,0:T(8,128)} %bitcast.2, f32[64,512]{1,0:T(8,128)} %get-tuple-element.8.y_ref), custom_call_target="tpu_custom_call" | custom-call | tf_op jit(solution)/shard_map/pallas_call | solution.py:585

commit v7 on v6

--- a/solution.py
+++ b/solution.py
@@ -363,9 +363,10 @@
         rows = pl.ds(to * 256, 256)
         block = (dot_nt(dense_re[rows, :], z_re[...]) - dot_nt(dense_im[rows, :], z_im[...])).reshape(4, 64, half)
         if d:
-            ysa[d - 1] = block.astype(ysa.dtype)
-            first_a[d] = remote(ysa.at[d - 1], yra.at[d - 1], sya.at[d - 1], rya.at[d - 1], r, to * 4 + y)
-            first_a[d].start()
+            for p in range(2):
+                ysa[p, d - 1] = block[:, :, p * 128 : p * 128 + 128].astype(ysa.dtype)
+                first_a[d, p] = remote(ysa.at[p, d - 1], yra.at[p, d - 1], sya.at[p, d - 1], rya.at[p, d - 1], r, to * 4 + y)
+                first_a[d, p].start()
         else:
             yown_a[...] = block
         to = (y + d) % 4
@@ -373,41 +374,41 @@
         rows_im = jnp.concatenate([dense_im[pl.ds(i * 256 + to * 64, 64), :] for i in range(4)], axis=0)
         block = (dot_nt(rows_re, z_im[...]) + dot_nt(rows_im, z_re[...])).reshape(4, 64, half)
         if d:
-            ysb[d - 1] = block.astype(ysb.dtype)
-            first_b[d] = remote(ysb.at[d - 1], yrb.at[d - 1], syb.at[d - 1], ryb.at[d - 1], r, x * 4 + to)
-            first_b[d].start()
+            for p in range(2):
+                ysb[p, d - 1] = block[:, :, p * 128 : p * 128 + 128].astype(ysb.dtype)
+                first_b[d, p] = remote(ysb.at[p, d - 1], yrb.at[p, d - 1], syb.at[p, d - 1], ryb.at[p, d - 1], r, x * 4 + to)
+                first_b[d, p].start()
         else:
             yown_b[...] = block
-    sum_a = yown_a[...]
-    for d in range(1, 4):
-        first_a[d].wait_recv()
-        sum_a = sum_a + yra[d - 1].astype(jnp.float32)
-    yown_a[...] = sum_a
-    ys2[0] = sum_a.astype(ys2.dtype)
-    second_a = []
-    for d in range(1, 4):
-        to = (y + d) % 4
-        second_a.append(remote(ys2.at[0, to], yr2a.at[d - 1], sy2a.at[d - 1], ry2a.at[d - 1], r, x * 4 + to))
-        second_a[-1].start()
-    sum_b = yown_b[...]
-    for d in range(1, 4):
-        first_b[d].wait_recv()
-        sum_b = sum_b + yrb[d - 1].astype(jnp.float32)
-    yown_b[...] = sum_b
-    ys2[1] = sum_b.astype(ys2.dtype)
-    second_b = []
-    for d in range(1, 4):
-        to = (x + d) % 4
-        second_b.append(remote(ys2.at[1, to], yr2b.at[d - 1], sy2b.at[d - 1], ry2b.at[d - 1], r, to * 4 + y))
-        second_b[-1].start()
-    final_a = yown_a[y]
-    for d in range(1, 4):
-        second_a[d - 1].wait_recv()
-        final_a = final_a + yr2a[d - 1].astype(jnp.float32)
-    final_b = yown_b[x]
-    for d in range(1, 4):
-        second_b[d - 1].wait_recv()
-        final_b = final_b + yr2b[d - 1].astype(jnp.float32)
+    second_a, second_b = {}, {}
+    for p in range(2):
+        lanes = pl.ds(p * 128, 128)
+        for k, own, first, got_ref, second, out_sem, in_sem, land in (
+            (0, yown_a, first_a, yra, second_a, sy2a, ry2a, yr2a),
+            (1, yown_b, first_b, yrb, second_b, sy2b, ry2b, yr2b),
+        ):
+            total = own[:, :, lanes]
+            for d in range(1, 4):
+                first[d, p].wait_recv()
+                total = total + got_ref[p, d - 1].astype(jnp.float32)
+            own[:, :, lanes] = total
+            ys2[k, p] = total.astype(ys2.dtype)
+            for d in range(1, 4):
+                to = (y + d) % 4 if k == 0 else (x + d) % 4
+                col = x * 4 + to if k == 0 else to * 4 + y
+                second[d, p] = remote(ys2.at[k, p, to], land.at[p, d - 1], out_sem.at[p, d - 1], in_sem.at[p, d - 1], r, col)
+                second[d, p].start()
+    pieces_a, pieces_b = [], []
+    for p in range(2):
+        lanes = pl.ds(p * 128, 128)
+        for pieces, own, mine, second, land in ((pieces_a, yown_a, y, second_a, yr2a), (pieces_b, yown_b, x, second_b, yr2b)):
+            total = own[mine, :, lanes]
+            for d in range(1, 4):
+                second[d, p].wait_recv()
+                total = total + land[p, d - 1].astype(jnp.float32)
+            pieces.append(total)
+    final_a = jnp.concatenate(pieces_a, axis=1)
+    final_b = jnp.concatenate(pieces_b, axis=1)
     image_ref[:, :half] = final_a
     image_ref[:, half:] = final_b
 
@@ -451,7 +452,7 @@
     for s in range(8):
         for copy in across[s] + back[s] + relay[s]:
             copy.wait_send()
-    for copy in swap + sends + spread + hand + list(first_a.values()) + list(first_b.values()) + second_a + second_b + g1 + g2 + g3:
+    for copy in swap + sends + spread + hand + list(first_a.values()) + list(first_b.values()) + list(second_a.values()) + list(second_b.values()) + g1 + g2 + g3:
         copy.wait_send()
 
 
@@ -466,12 +467,12 @@
         vm((4, 32, 512), bf), vm((4, 32, 512), bf), vm((4, 32, 512), bf), vm((3, 32, 512), bf),
         vm((2, 1024, 512), f32), vm((1024, 512), bf), vm((1024, 512), bf),
         vm((2, RANK, 1024), bf), vm((256, 512), f32), vm((256, 512), bf), vm((256, 512), bf), vm((2, 4, 32, 512), bf), vm((2, 3, 32, 512), bf), vm((512, 512), bf),
-        vm((4, 64, 256), f32), vm((4, 64, 256), f32), vm((3, 4, 64, 256), bf), vm((3, 4, 64, 256), bf),
-        vm((3, 4, 64, 256), bf), vm((3, 4, 64, 256), bf), vm((2, 4, 64, 256), bf), vm((3, 64, 256), bf), vm((3, 64, 256), bf),
+        vm((4, 64, 256), f32), vm((4, 64, 256), f32), vm((2, 3, 4, 64, 128), bf), vm((2, 3, 4, 64, 128), bf),
+        vm((2, 3, 4, 64, 128), bf), vm((2, 3, 4, 64, 128), bf), vm((2, 2, 4, 64, 128), bf), vm((2, 3, 64, 128), bf), vm((2, 3, 64, 128), bf),
         vm((16, 16, RANK), f32), vm((15, 16, RANK), f32), vm((8, 16, RANK), f32),
         dma((3,)), dma((40,)), dma((40,)), dma((8,)), dma((8,)), dma((8, 3)), dma((8, 3)), dma((8, 3)), dma((8, 3)), dma((8, 4)), dma((8, 4)),
-        dma((2,)), dma((2,)), dma((2, 3)), dma((2, 3)), dma((2, 3)), dma((2, 3)), dma((2, 4)), dma((2, 4)), dma((3,)), dma((3,)), dma((3,)), dma((3,)),
-        dma((3,)), dma((3,)), dma((3,)), dma((3,)), dma((15,)), dma((15,)), dma((7,)), dma((7,)), dma((15,)), dma((15,)),
+        dma((2,)), dma((2,)), dma((2, 3)), dma((2, 3)), dma((2, 3)), dma((2, 3)), dma((2, 4)), dma((2, 4)), dma((2, 3)), dma((2, 3)), dma((2, 3)), dma((2, 3)),
+        dma((2, 3)), dma((2, 3)), dma((2, 3)), dma((2, 3)), dma((15,)), dma((15,)), dma((7,)), dma((7,)), dma((15,)), dma((15,)),
     ]
     return pl.pallas_call(
         front_kernel,

time: 134 us -> 134 us (level)
  no operation moved by 1% of the time
where the time goes in v7:
time: 134 us
  Pallas kernels  134 us (100%)
    pallas_call x1, Pallas kernels, front(): pl.pallas_call(front_kernel, out_shape=(jax.ShapeDtypeStruct((64, 2 * RAN...  119 us
    pallas_call x1, Pallas kernels, chol(): pl.pallas_call(functools.partial(chol_kernel, scale), out_shape=jax.Shape...  14.9 us

profile of v7, /device:TPU:0, one launch (start us, length us, event | category | flops | bytes accessed | tf_op | source)
XLA Modules:
  0.0 133.9 jit_solution(12155429525092990172)
XLA Ops:
  0.0 118.9 %shard_map.64 = (f32[64,512]{1,0:T(8,128)}, f32[16,16,256]{2,1,0:T(8,128)}) custom-call(bf16[2,64,2048]{2,1,0:T(8,128)(2,1)} %refl_ref.1, s32[1,2048]{1,0:T(1,128)} %bitcast.3, bf16[1024,2,256]{2,1,0:T(2,128)(2,1)} %q_ref.1, bf16[2,2048,512]{2,1,0:T(8,128)(2,1)} %focus_in_hbm.1, bf16[2,1024,1024]{2,1,0:T(8,128)(2,1)} %focus_out_hbm.1, f32[1024,512]{1,0:T(8,128)} %angle_hbm.1), custom_call_target="tpu_custom_call" | custom-call | tf_op jit(solution)/shard_map/pallas_call | solution.py:477
  118.9 14.9 %shard_map.65 = f32[64,2,256]{2,1,0:T(2,128)} custom-call(f32[256,256]{1,0:T(8,128)} %bitcast.2, f32[64,512]{1,0:T(8,128)} %get-tuple-element.8.y_ref), custom_call_target="tpu_custom_call" | custom-call | tf_op jit(solution)/shard_map/pallas_call | solution.py:586
